TPU v7x, 512 devices: a whole 4x4x16 slice. The times are simulated.
512 devices in a mesh: shot: 16 (over x, z_lo), tx: 8 (over z_hi, core), ty: 4 (over y).
Axes of the slice: x: 4, y: 4, z: 16 (z_hi: 4, z_lo: 4; z = z_hi * 4 + z_lo), core: 2. Of those that a mesh axis runs over, the one named last changes fastest.
Arguments:
- adjoint_prior: float32 [16, 32, 256, 512], P('shot', None, 'tx', 'ty'), may hold values from -6 to 6
- adjoint_now: float32 [16, 32, 256, 512], P('shot', None, 'tx', 'ty'), may hold values from -6 to 6
- forward_saved: float32 [16, 2, 32, 256, 512], P('shot', None, None, 'tx', 'ty'), may hold values from -6 to 6
- residuals: float32 [16, 10, 1024], P('shot'), may hold values from -6 to 6
- receiver_x: int32 [16, 1024], P('shot'), may hold values from 0 to 255
- receiver_y: int32 [16, 1024], P('shot'), may hold values from 0 to 511
- source_x: int32 [16], P('shot'), may hold values from 0 to 255
- source_y: int32 [16], P('shot'), may hold values from 0 to 511
- saved_slot: int32 [10], replicated, may hold values from 0 to 1
- model: float32 [32, 256, 512], P('shot', 'tx', 'ty'), may hold values from 0.03 to 0.12
Outputs:
- adjoint_state: float32 [16, 32, 256, 512], P('shot', None, 'tx', 'ty')
- gradient: float32 [32, 256, 512], P('shot', 'tx', 'ty')
- updated_model: float32 [32, 256, 512], P('shot', 'tx', 'ty')
All inputs are finite; a program needn't handle non-finite values.
Results may differ from a plain program's by a relative error of at most 0.0001.
Values sent between devices are 32-bit elements; how exact they have to be, the bound alone decides.
A program may use at most 64 MiB of HBM per device.

v0:
```python
import math

import jax
import jax.numpy as jnp
from jax import lax
from jax.sharding import PartitionSpec as P

STEPS = 10


rec_depth = 2
src_depth = 3.0
mute_radius = 10.0
step_size = 0.01


def with_halo(cells, sides, width):
    for axis, dim in sides:
        count = lax.axis_size(axis)
        ends = count - 1
        head = lax.slice_in_dim(cells, 0, width, axis=dim)
        tail = lax.slice_in_dim(cells, cells.shape[dim] - width, cells.shape[dim], axis=dim)
        cells = jnp.concatenate(
            [
                lax.ppermute(tail, axis, [(i, (i + 1) % count) for i in range(ends)]),
                cells,
                lax.ppermute(head, axis, [((i + 1) % count, i) for i in range(ends)]),
            ],
            axis=dim,
        )
    return cells


def coefficients():
    weights_table = []
    for offset in range(1, 9):
        weights_table.append(
            2.0
            * (-1.0) ** (offset + 1)
            * math.factorial(8) ** 2
            / (offset * offset * math.factorial(8 - offset) * math.factorial(8 + offset))
        )
    centre = -2.0 * sum(weights_table)
    return (centre, weights_table)


def laplace(padded):
    centre, weights_table = coefficients()
    span_x = padded.shape[-2] - 16
    span_y = padded.shape[-1] - 16
    depth_cells = padded.shape[-3]
    interior = padded[..., 8 : 8 + span_x, 8 : 8 + span_y]
    pad_spec = [(0, 0)] * (padded.ndim - 3) + [(8, 8), (0, 0), (0, 0)]
    column = jnp.pad(interior, pad_spec)
    summed = 3.0 * centre * interior
    for offset in range(1, 9):
        weight = weights_table[offset - 1]
        neighbours = (
            padded[..., 8 + offset : 8 + offset + span_x, 8 : 8 + span_y]
            + padded[..., 8 - offset : 8 - offset + span_x, 8 : 8 + span_y]
        )
        neighbours = (
            neighbours
            + padded[..., 8 : 8 + span_x, 8 + offset : 8 + offset + span_y]
            + padded[..., 8 : 8 + span_x, 8 - offset : 8 - offset + span_y]
        )
        neighbours = (
            neighbours
            + column[..., 8 + offset : 8 + offset + depth_cells, :, :]
            + column[..., 8 - offset : 8 - offset + depth_cells, :, :]
        )
        summed = summed + weight * neighbours
    return summed


def inject(field_block, traces, rec_x, rec_y, start_x, start_y):
    shots_here, depth_cells, span_x, span_y = field_block.shape
    local_x = rec_x - start_x
    local_y = rec_y - start_y
    inside = (local_x >= 0) & (local_x < span_x) & (local_y >= 0) & (local_y < span_y)
    flat_index = (
        jnp.arange(shots_here, dtype=jnp.int32)[:, None] * (span_x * span_y)
        + local_x * span_y
        + local_y
    )
    flat_index = jnp.where(inside, flat_index, shots_here * span_x * span_y)
    surface = (
        jnp.zeros((shots_here * span_x * span_y,), jnp.float32)
        .at[flat_index.reshape(-1)]
        .add(traces.reshape(-1), mode="drop")
    )
    return field_block.at[:, rec_depth].add(surface.reshape(shots_here, span_x, span_y))


def shards(
    adjoint_prior,
    adjoint_now,
    forward_saved,
    residuals,
    receiver_x,
    receiver_y,
    source_x,
    source_y,
    saved_slot,
    model,
):
    shots_here, depth_cells, span_x, span_y = adjoint_now.shape
    anchor_x = lax.axis_index("tx") * span_x
    anchor_y = lax.axis_index("ty") * span_y
    velocity = lax.all_gather(model, "shot", axis=0, tiled=True)

    def snapshot_at(moment):
        return lax.dynamic_index_in_dim(forward_saved, saved_slot[moment], 1, keepdims=False)

    def traces_at(moment):
        return lax.dynamic_index_in_dim(residuals, moment, 1, keepdims=False)

    imaging = jnp.zeros_like(adjoint_now)

    def one_step(step_index, state_carry):
        previous, current, image_sum = state_carry
        moment = STEPS - 1 - step_index
        padded = with_halo(current, (("tx", 2), ("ty", 3)), 8)
        updated = 2.0 * current - previous + velocity * laplace(padded)
        updated = inject(updated, traces_at(moment), receiver_x, receiver_y, anchor_x, anchor_y)
        image_sum = image_sum + snapshot_at(moment) * updated
        return (current, updated, image_sum)

    previous, current, imaging = lax.fori_loop(
        0, STEPS, one_step, (adjoint_prior, adjoint_now, imaging)
    )
    cells_z = jnp.arange(depth_cells, dtype=jnp.float32) - src_depth
    cells_x = (anchor_x + jnp.arange(span_x, dtype=jnp.int32)).astype(jnp.float32)
    cells_y = (anchor_y + jnp.arange(span_y, dtype=jnp.int32)).astype(jnp.float32)
    gap_x = cells_x[None, :] - source_x.astype(jnp.float32)[:, None]
    gap_y = cells_y[None, :] - source_y.astype(jnp.float32)[:, None]
    distance = (
        (cells_z * cells_z)[None, :, None, None]
        + (gap_x * gap_x)[:, None, :, None]
        + (gap_y * gap_y)[:, None, None, :]
    )
    mute_factor = 1.0 - jnp.exp(-distance / (mute_radius * mute_radius))
    weighted = jnp.sum(mute_factor * imaging, axis=0)
    summed_share = lax.psum_scatter(weighted, "shot", scatter_dimension=0, tiled=True)
    grad_scale = 1.0 / math.sqrt(shots_here * lax.axis_size("shot") * STEPS)
    gradient = summed_share * grad_scale
    updated_model = model - step_size * gradient
    return (current, gradient, updated_model)


def solution(mesh):
    return jax.shard_map(
        shards,
        mesh=mesh,
        in_specs=(
            P("shot", None, "tx", "ty"),
            P("shot", None, "tx", "ty"),
            P("shot", None, None, "tx", "ty"),
            P("shot", None, None),
            P("shot", None),
            P("shot", None),
            P("shot"),
            P("shot"),
            P(),
            P("shot", "tx", "ty"),
        ),
        out_specs=(P("shot", None, "tx", "ty"), P("shot", "tx", "ty"), P("shot", "tx", "ty")),
        check_vma=False,
    )
```

profile of v0, /device:TPU:24, one launch (start us, length us, event | category | flops | bytes accessed | tf_op | source)
XLA Modules:
  0.0 605.6 jit_solution(2568450750883470735)
XLA Ops:
  9.1 50.9 %all_gather.3 = f32[32,32,128]{2,1,0:T(8,128)} all-gather(f32[2,32,128]{2,1,0:T(8,128)S(1)} %copy-done.5), channel_id=1, replica_groups=mesh['shot'=16,'tx'=8,'ty'=4] {'shot'}, dimensions={0}, use_global_device_ids=true | all-gather | bytes 557056 | tf_op jit(solution)/shard_map/all_gather | solution.py:110
  62.6 441.1 %while.21 = (s32[]{:T(128)}, f32[1,32,32,128]{3,2,1,0:T(8,128)}, f32[1,32,32,128]{3,2,1,0:T(8,128)S(1)}, f32[1,32,32,128]{3,2,1,0:T(8,128)}, f32[32,32,128]{2,1,...) while((s32[]{:T(128)}, f32[1,32,32,128]{3,2,1,0:T(8,128)}, ...), condition=%wide.region_2.3_spmd.clone, body=%wide.region_0.2_spmd.clone.sunk | while | flops 10506250 | bytes 29512980 | solution.py:129
  66.0 8.6 %collective-permute-done.1 = f32[1,32,8,128]{3,2,1,0:T(8,128)S(1)} collective-permute-done((f32[1,32,8,128]{3,2,1,0:T(8,128)S(1)}, f32[1,32,8,128]{3,2,1,0:T(8,128)S(1)}, u32[]{:S(2)}, u32[]{:S(2)}) %collective-permute-start.1) | collective-permute-done | bytes 131104 | tf_op jit(solution)/shard_map/while/body/eval_jaxpr/ppermute | solution.py:27
  87.5 6.1 scatter_custom_fusion.6
  96.9 7.1 %fusion.79 = f32[1,32,32,128]{3,2,1,0:T(8,128)S(1)} fusion(f32[1,32,32,128]{3,2,1,0:T(8,128)S(1)} %get-tuple-element.525, f32[1,32,48,8]{3,2,1,0:T(8,128)S(1)} %copy.28, f32[1,32,48,128]{3,2,1,0:T(8,128)S(1)} %get-tuple-element.500, f32[1,32,48,8]{3,2,1,0:T(8,128)} %copy.30, f32[1,32,40,128]{3,2,1,0:T(8,128)S(1)} %get-tuple-element.503, ...), kind=kLoop, calls=%fused_computation.57.clone.1 | loop fusion | flops 10092544 | bytes 11370496 | tf_op jit(solution)/shard_map/while/body/eval_jaxpr/add | solution.py:124
  106.7 8.8 %collective-permute-start = (f32[1,32,8,128]{3,2,1,0:T(8,128)S(1)}, f32[1,32,8,128]{3,2,1,0:T(8,128)S(1)}, u32[]{:S(2)}, u32[]{:S(2)}) collective-permute-start(f32[1,32,8,128]{3,2,1,0:T(8,128)S(1)} %get-tuple-element.494), channel_id=1, source_target_pairs={{0,4},{4,8},{8,12},{12,16},{16,20},{20,24},{24,28},{1,5},{5,9},{9,... | collective-permute-start | bytes 393224 | tf_op jit(solution)/shard_map/while/body/eval_jaxpr/ppermute | solution.py:25
  141.0 7.1 %fusion.79 = f32[1,32,32,128]{3,2,1,0:T(8,128)S(1)} fusion(f32[1,32,32,128]{3,2,1,0:T(8,128)S(1)} %get-tuple-element.525, f32[1,32,48,8]{3,2,1,0:T(8,128)S(1)} %copy.28, f32[1,32,48,128]{3,2,1,0:T(8,128)S(1)} %get-tuple-element.500, f32[1,32,48,8]{3,2,1,0:T(8,128)} %copy.30, f32[1,32,40,128]{3,2,1,0:T(8,128)S(1)} %get-tuple-element.503, ...), kind=kLoop, calls=%fused_computation.57.clone.1 | loop fusion | flops 10092544 | bytes 11370496 | tf_op jit(solution)/shard_map/while/body/eval_jaxpr/add | solution.py:124
  150.9 8.7 %collective-permute-start = (f32[1,32,8,128]{3,2,1,0:T(8,128)S(1)}, f32[1,32,8,128]{3,2,1,0:T(8,128)S(1)}, u32[]{:S(2)}, u32[]{:S(2)}) collective-permute-start(f32[1,32,8,128]{3,2,1,0:T(8,128)S(1)} %get-tuple-element.494), channel_id=1, source_target_pairs={{0,4},{4,8},{8,12},{12,16},{16,20},{20,24},{24,28},{1,5},{5,9},{9,... | collective-permute-start | bytes 393224 | tf_op jit(solution)/shard_map/while/body/eval_jaxpr/ppermute | solution.py:25
  175.8 6.1 scatter_custom_fusion.6
  185.1 7.1 %fusion.79 = f32[1,32,32,128]{3,2,1,0:T(8,128)S(1)} fusion(f32[1,32,32,128]{3,2,1,0:T(8,128)S(1)} %get-tuple-element.525, f32[1,32,48,8]{3,2,1,0:T(8,128)S(1)} %copy.28, f32[1,32,48,128]{3,2,1,0:T(8,128)S(1)} %get-tuple-element.500, f32[1,32,48,8]{3,2,1,0:T(8,128)} %copy.30, f32[1,32,40,128]{3,2,1,0:T(8,128)S(1)} %get-tuple-element.503, ...), kind=kLoop, calls=%fused_computation.57.clone.1 | loop fusion | flops 10092544 | bytes 11370496 | tf_op jit(solution)/shard_map/while/body/eval_jaxpr/add | solution.py:124
  195.0 8.7 %collective-permute-start = (f32[1,32,8,128]{3,2,1,0:T(8,128)S(1)}, f32[1,32,8,128]{3,2,1,0:T(8,128)S(1)}, u32[]{:S(2)}, u32[]{:S(2)}) collective-permute-start(f32[1,32,8,128]{3,2,1,0:T(8,128)S(1)} %get-tuple-element.494), channel_id=1, source_target_pairs={{0,4},{4,8},{8,12},{12,16},{16,20},{20,24},{24,28},{1,5},{5,9},{9,... | collective-permute-start | bytes 393224 | tf_op jit(solution)/shard_map/while/body/eval_jaxpr/ppermute | solution.py:25
  219.9 6.1 scatter_custom_fusion.6
  229.2 7.1 %fusion.79 = f32[1,32,32,128]{3,2,1,0:T(8,128)S(1)} fusion(f32[1,32,32,128]{3,2,1,0:T(8,128)S(1)} %get-tuple-element.525, f32[1,32,48,8]{3,2,1,0:T(8,128)S(1)} %copy.28, f32[1,32,48,128]{3,2,1,0:T(8,128)S(1)} %get-tuple-element.500, f32[1,32,48,8]{3,2,1,0:T(8,128)} %copy.30, f32[1,32,40,128]{3,2,1,0:T(8,128)S(1)} %get-tuple-element.503, ...), kind=kLoop, calls=%fused_computation.57.clone.1 | loop fusion | flops 10092544 | bytes 11370496 | tf_op jit(solution)/shard_map/while/body/eval_jaxpr/add | solution.py:124
  239.1 8.7 %collective-permute-start = (f32[1,32,8,128]{3,2,1,0:T(8,128)S(1)}, f32[1,32,8,128]{3,2,1,0:T(8,128)S(1)}, u32[]{:S(2)}, u32[]{:S(2)}) collective-permute-start(f32[1,32,8,128]{3,2,1,0:T(8,128)S(1)} %get-tuple-element.494), channel_id=1, source_target_pairs={{0,4},{4,8},{8,12},{12,16},{16,20},{20,24},{24,28},{1,5},{5,9},{9,... | collective-permute-start | bytes 393224 | tf_op jit(solution)/shard_map/while/body/eval_jaxpr/ppermute | solution.py:25
  264.0 6.1 scatter_custom_fusion.6
  273.3 7.1 %fusion.79 = f32[1,32,32,128]{3,2,1,0:T(8,128)S(1)} fusion(f32[1,32,32,128]{3,2,1,0:T(8,128)S(1)} %get-tuple-element.525, f32[1,32,48,8]{3,2,1,0:T(8,128)S(1)} %copy.28, f32[1,32,48,128]{3,2,1,0:T(8,128)S(1)} %get-tuple-element.500, f32[1,32,48,8]{3,2,1,0:T(8,128)} %copy.30, f32[1,32,40,128]{3,2,1,0:T(8,128)S(1)} %get-tuple-element.503, ...), kind=kLoop, calls=%fused_computation.57.clone.1 | loop fusion | flops 10092544 | bytes 11370496 | tf_op jit(solution)/shard_map/while/body/eval_jaxpr/add | solution.py:124
  283.2 8.7 %collective-permute-start = (f32[1,32,8,128]{3,2,1,0:T(8,128)S(1)}, f32[1,32,8,128]{3,2,1,0:T(8,128)S(1)}, u32[]{:S(2)}, u32[]{:S(2)}) collective-permute-start(f32[1,32,8,128]{3,2,1,0:T(8,128)S(1)} %get-tuple-element.494), channel_id=1, source_target_pairs={{0,4},{4,8},{8,12},{12,16},{16,20},{20,24},{24,28},{1,5},{5,9},{9,... | collective-permute-start | bytes 393224 | tf_op jit(solution)/shard_map/while/body/eval_jaxpr/ppermute | solution.py:25
  308.1 6.1 scatter_custom_fusion.6
  317.5 7.1 %fusion.79 = f32[1,32,32,128]{3,2,1,0:T(8,128)S(1)} fusion(f32[1,32,32,128]{3,2,1,0:T(8,128)S(1)} %get-tuple-element.525, f32[1,32,48,8]{3,2,1,0:T(8,128)S(1)} %copy.28, f32[1,32,48,128]{3,2,1,0:T(8,128)S(1)} %get-tuple-element.500, f32[1,32,48,8]{3,2,1,0:T(8,128)} %copy.30, f32[1,32,40,128]{3,2,1,0:T(8,128)S(1)} %get-tuple-element.503, ...), kind=kLoop, calls=%fused_computation.57.clone.1 | loop fusion | flops 10092544 | bytes 11370496 | tf_op jit(solution)/shard_map/while/body/eval_jaxpr/add | solution.py:124
  327.3 8.7 %collective-permute-start = (f32[1,32,8,128]{3,2,1,0:T(8,128)S(1)}, f32[1,32,8,128]{3,2,1,0:T(8,128)S(1)}, u32[]{:S(2)}, u32[]{:S(2)}) collective-permute-start(f32[1,32,8,128]{3,2,1,0:T(8,128)S(1)} %get-tuple-element.494), channel_id=1, source_target_pairs={{0,4},{4,8},{8,12},{12,16},{16,20},{20,24},{24,28},{1,5},{5,9},{9,... | collective-permute-start | bytes 393224 | tf_op jit(solution)/shard_map/while/body/eval_jaxpr/ppermute | solution.py:25
  352.2 6.1 scatter_custom_fusion.6
  361.6 7.1 %fusion.79 = f32[1,32,32,128]{3,2,1,0:T(8,128)S(1)} fusion(f32[1,32,32,128]{3,2,1,0:T(8,128)S(1)} %get-tuple-element.525, f32[1,32,48,8]{3,2,1,0:T(8,128)S(1)} %copy.28, f32[1,32,48,128]{3,2,1,0:T(8,128)S(1)} %get-tuple-element.500, f32[1,32,48,8]{3,2,1,0:T(8,128)} %copy.30, f32[1,32,40,128]{3,2,1,0:T(8,128)S(1)} %get-tuple-element.503, ...), kind=kLoop, calls=%fused_computation.57.clone.1 | loop fusion | flops 10092544 | bytes 11370496 | tf_op jit(solution)/shard_map/while/body/eval_jaxpr/add | solution.py:124
  371.4 8.7 %collective-permute-start = (f32[1,32,8,128]{3,2,1,0:T(8,128)S(1)}, f32[1,32,8,128]{3,2,1,0:T(8,128)S(1)}, u32[]{:S(2)}, u32[]{:S(2)}) collective-permute-start(f32[1,32,8,128]{3,2,1,0:T(8,128)S(1)} %get-tuple-element.494), channel_id=1, source_target_pairs={{0,4},{4,8},{8,12},{12,16},{16,20},{20,24},{24,28},{1,5},{5,9},{9,... | collective-permute-start | bytes 393224 | tf_op jit(solution)/shard_map/while/body/eval_jaxpr/ppermute | solution.py:25
  396.3 6.1 scatter_custom_fusion.6
  405.7 7.1 %fusion.79 = f32[1,32,32,128]{3,2,1,0:T(8,128)S(1)} fusion(f32[1,32,32,128]{3,2,1,0:T(8,128)S(1)} %get-tuple-element.525, f32[1,32,48,8]{3,2,1,0:T(8,128)S(1)} %copy.28, f32[1,32,48,128]{3,2,1,0:T(8,128)S(1)} %get-tuple-element.500, f32[1,32,48,8]{3,2,1,0:T(8,128)} %copy.30, f32[1,32,40,128]{3,2,1,0:T(8,128)S(1)} %get-tuple-element.503, ...), kind=kLoop, calls=%fused_computation.57.clone.1 | loop fusion | flops 10092544 | bytes 11370496 | tf_op jit(solution)/shard_map/while/body/eval_jaxpr/add | solution.py:124
  415.5 8.7 %collective-permute-start = (f32[1,32,8,128]{3,2,1,0:T(8,128)S(1)}, f32[1,32,8,128]{3,2,1,0:T(8,128)S(1)}, u32[]{:S(2)}, u32[]{:S(2)}) collective-permute-start(f32[1,32,8,128]{3,2,1,0:T(8,128)S(1)} %get-tuple-element.494), channel_id=1, source_target_pairs={{0,4},{4,8},{8,12},{12,16},{16,20},{20,24},{24,28},{1,5},{5,9},{9,... | collective-permute-start | bytes 393224 | tf_op jit(solution)/shard_map/while/body/eval_jaxpr/ppermute | solution.py:25
  440.4 6.1 scatter_custom_fusion.6
  449.8 7.1 %fusion.79 = f32[1,32,32,128]{3,2,1,0:T(8,128)S(1)} fusion(f32[1,32,32,128]{3,2,1,0:T(8,128)S(1)} %get-tuple-element.525, f32[1,32,48,8]{3,2,1,0:T(8,128)S(1)} %copy.28, f32[1,32,48,128]{3,2,1,0:T(8,128)S(1)} %get-tuple-element.500, f32[1,32,48,8]{3,2,1,0:T(8,128)} %copy.30, f32[1,32,40,128]{3,2,1,0:T(8,128)S(1)} %get-tuple-element.503, ...), kind=kLoop, calls=%fused_computation.57.clone.1 | loop fusion | flops 10092544 | bytes 11370496 | tf_op jit(solution)/shard_map/while/body/eval_jaxpr/add | solution.py:124
  459.6 8.7 %collective-permute-start = (f32[1,32,8,128]{3,2,1,0:T(8,128)S(1)}, f32[1,32,8,128]{3,2,1,0:T(8,128)S(1)}, u32[]{:S(2)}, u32[]{:S(2)}) collective-permute-start(f32[1,32,8,128]{3,2,1,0:T(8,128)S(1)} %get-tuple-element.494), channel_id=1, source_target_pairs={{0,4},{4,8},{8,12},{12,16},{16,20},{20,24},{24,28},{1,5},{5,9},{9,... | collective-permute-start | bytes 393224 | tf_op jit(solution)/shard_map/while/body/eval_jaxpr/ppermute | solution.py:25
  484.5 6.1 scatter_custom_fusion.6
  493.9 7.1 %fusion.79 = f32[1,32,32,128]{3,2,1,0:T(8,128)S(1)} fusion(f32[1,32,32,128]{3,2,1,0:T(8,128)S(1)} %get-tuple-element.525, f32[1,32,48,8]{3,2,1,0:T(8,128)S(1)} %copy.28, f32[1,32,48,128]{3,2,1,0:T(8,128)S(1)} %get-tuple-element.500, f32[1,32,48,8]{3,2,1,0:T(8,128)} %copy.30, f32[1,32,40,128]{3,2,1,0:T(8,128)S(1)} %get-tuple-element.503, ...), kind=kLoop, calls=%fused_computation.57.clone.1 | loop fusion | flops 10092544 | bytes 11370496 | tf_op jit(solution)/shard_map/while/body/eval_jaxpr/add | solution.py:124
  506.0 91.4 %reduce-scatter.2.cloned.1.call-done = f32[2,32,128]{2,1,0:T(8,128)} async-done(((f32[32,32,128]{2,1,0:T(8,128)}), f32[2,32,128]{2,1,0:T(8,128)}) %reduce-scatter.2.cloned.1.call-update) | async-done | bytes 32784 | tf_op jit(solution)/shard_map/reduce_scatter | solution.py:144
  (374 shorter events, 217.1 us)
Async XLA Ops:
  7.2 590.2 %reduce-scatter.2.cloned.1.call-start = ((), (), s32[]{:S(2)}) async-start(), calls=%async_computation.1 | async-start | bytes 557056 | tf_op jit(solution)/shard_map/reduce_scatter | solution.py:144
  63.9 10.7 %collective-permute-start.1 = (f32[1,32,8,128]{3,2,1,0:T(8,128)S(1)}, f32[1,32,8,128]{3,2,1,0:T(8,128)S(1)}, u32[]{:S(2)}, u32[]{:S(2)}) collective-permute-start(f32[1,32,8,128]{3,2,1,0:T(8,128)S(1)} %get-tuple-element.498), channel_id=1, source_target_pairs={{4,0},{8,4},{12,8},{16,12},{20,16},{24,20},{28,24},{5,1},{9,5},{13... | collective-permute-start | bytes 393224 | tf_op jit(solution)/shard_map/while/body/eval_jaxpr/ppermute | solution.py:27
  77.1 16.5 %collective-permute-start.2 = (f32[1,32,48,8]{2,3,1,0:T(8,128)S(1)}, f32[1,32,48,8]{2,3,1,0:T(8,128)}, u32[]{:S(2)}, u32[]{:S(2)}) collective-permute-start(f32[1,32,48,8]{2,3,1,0:T(8,128)S(1)} %copy.27), channel_id=1, source_target_pairs={{0,1},{1,2},{2,3},{4,5},{5,6},{6,7},{8,9},{9,10},{10,11},{12,13},{... | collective-permute-start | bytes 147464 | tf_op jit(solution)/shard_map/while/body/eval_jaxpr/ppermute | solution.py:25
  79.3 15.4 %collective-permute-start.3 = (f32[1,32,48,8]{2,3,1,0:T(8,128)}, f32[1,32,48,8]{2,3,1,0:T(8,128)}, u32[]{:S(2)}, u32[]{:S(2)}) collective-permute-start(f32[1,32,48,8]{2,3,1,0:T(8,128)} %copy.29), channel_id=1, source_target_pairs={{1,0},{2,1},{3,2},{5,4},{6,5},{7,6},{9,8},{10,9},{11,10},{13,12},{... | collective-permute-start | bytes 147464 | tf_op jit(solution)/shard_map/while/body/eval_jaxpr/ppermute | solution.py:27
  106.7 10.7 %collective-permute-start = (f32[1,32,8,128]{3,2,1,0:T(8,128)S(1)}, f32[1,32,8,128]{3,2,1,0:T(8,128)S(1)}, u32[]{:S(2)}, u32[]{:S(2)}) collective-permute-start(f32[1,32,8,128]{3,2,1,0:T(8,128)S(1)} %get-tuple-element.494), channel_id=1, source_target_pairs={{0,4},{4,8},{8,12},{12,16},{16,20},{20,24},{24,28},{1,5},{5,9},{9,... | collective-permute-start | bytes 393224 | tf_op jit(solution)/shard_map/while/body/eval_jaxpr/ppermute | solution.py:25
  115.5 3.2 collective-permute-start.1
  121.3 16.5 %collective-permute-start.2 = (f32[1,32,48,8]{2,3,1,0:T(8,128)S(1)}, f32[1,32,48,8]{2,3,1,0:T(8,128)}, u32[]{:S(2)}, u32[]{:S(2)}) collective-permute-start(f32[1,32,48,8]{2,3,1,0:T(8,128)S(1)} %copy.27), channel_id=1, source_target_pairs={{0,1},{1,2},{2,3},{4,5},{5,6},{6,7},{8,9},{9,10},{10,11},{12,13},{... | collective-permute-start | bytes 147464 | tf_op jit(solution)/shard_map/while/body/eval_jaxpr/ppermute | solution.py:25
  123.5 15.4 %collective-permute-start.3 = (f32[1,32,48,8]{2,3,1,0:T(8,128)}, f32[1,32,48,8]{2,3,1,0:T(8,128)}, u32[]{:S(2)}, u32[]{:S(2)}) collective-permute-start(f32[1,32,48,8]{2,3,1,0:T(8,128)} %copy.29), channel_id=1, source_target_pairs={{1,0},{2,1},{3,2},{5,4},{6,5},{7,6},{9,8},{10,9},{11,10},{13,12},{... | collective-permute-start | bytes 147464 | tf_op jit(solution)/shard_map/while/body/eval_jaxpr/ppermute | solution.py:27
  150.9 10.7 %collective-permute-start = (f32[1,32,8,128]{3,2,1,0:T(8,128)S(1)}, f32[1,32,8,128]{3,2,1,0:T(8,128)S(1)}, u32[]{:S(2)}, u32[]{:S(2)}) collective-permute-start(f32[1,32,8,128]{3,2,1,0:T(8,128)S(1)} %get-tuple-element.494), channel_id=1, source_target_pairs={{0,4},{4,8},{8,12},{12,16},{16,20},{20,24},{24,28},{1,5},{5,9},{9,... | collective-permute-start | bytes 393224 | tf_op jit(solution)/shard_map/while/body/eval_jaxpr/ppermute | solution.py:25
  165.4 16.5 %collective-permute-start.2 = (f32[1,32,48,8]{2,3,1,0:T(8,128)S(1)}, f32[1,32,48,8]{2,3,1,0:T(8,128)}, u32[]{:S(2)}, u32[]{:S(2)}) collective-permute-start(f32[1,32,48,8]{2,3,1,0:T(8,128)S(1)} %copy.27), channel_id=1, source_target_pairs={{0,1},{1,2},{2,3},{4,5},{5,6},{6,7},{8,9},{9,10},{10,11},{12,13},{... | collective-permute-start | bytes 147464 | tf_op jit(solution)/shard_map/while/body/eval_jaxpr/ppermute | solution.py:25
  167.6 15.4 %collective-permute-start.3 = (f32[1,32,48,8]{2,3,1,0:T(8,128)}, f32[1,32,48,8]{2,3,1,0:T(8,128)}, u32[]{:S(2)}, u32[]{:S(2)}) collective-permute-start(f32[1,32,48,8]{2,3,1,0:T(8,128)} %copy.29), channel_id=1, source_target_pairs={{1,0},{2,1},{3,2},{5,4},{6,5},{7,6},{9,8},{10,9},{11,10},{13,12},{... | collective-permute-start | bytes 147464 | tf_op jit(solution)/shard_map/while/body/eval_jaxpr/ppermute | solution.py:27
  195.0 10.7 %collective-permute-start = (f32[1,32,8,128]{3,2,1,0:T(8,128)S(1)}, f32[1,32,8,128]{3,2,1,0:T(8,128)S(1)}, u32[]{:S(2)}, u32[]{:S(2)}) collective-permute-start(f32[1,32,8,128]{3,2,1,0:T(8,128)S(1)} %get-tuple-element.494), channel_id=1, source_target_pairs={{0,4},{4,8},{8,12},{12,16},{16,20},{20,24},{24,28},{1,5},{5,9},{9,... | collective-permute-start | bytes 393224 | tf_op jit(solution)/shard_map/while/body/eval_jaxpr/ppermute | solution.py:25
  209.5 16.5 %collective-permute-start.2 = (f32[1,32,48,8]{2,3,1,0:T(8,128)S(1)}, f32[1,32,48,8]{2,3,1,0:T(8,128)}, u32[]{:S(2)}, u32[]{:S(2)}) collective-permute-start(f32[1,32,48,8]{2,3,1,0:T(8,128)S(1)} %copy.27), channel_id=1, source_target_pairs={{0,1},{1,2},{2,3},{4,5},{5,6},{6,7},{8,9},{9,10},{10,11},{12,13},{... | collective-permute-start | bytes 147464 | tf_op jit(solution)/shard_map/while/body/eval_jaxpr/ppermute | solution.py:25
  211.7 15.4 %collective-permute-start.3 = (f32[1,32,48,8]{2,3,1,0:T(8,128)}, f32[1,32,48,8]{2,3,1,0:T(8,128)}, u32[]{:S(2)}, u32[]{:S(2)}) collective-permute-start(f32[1,32,48,8]{2,3,1,0:T(8,128)} %copy.29), channel_id=1, source_target_pairs={{1,0},{2,1},{3,2},{5,4},{6,5},{7,6},{9,8},{10,9},{11,10},{13,12},{... | collective-permute-start | bytes 147464 | tf_op jit(solution)/shard_map/while/body/eval_jaxpr/ppermute | solution.py:27
  239.1 10.7 %collective-permute-start = (f32[1,32,8,128]{3,2,1,0:T(8,128)S(1)}, f32[1,32,8,128]{3,2,1,0:T(8,128)S(1)}, u32[]{:S(2)}, u32[]{:S(2)}) collective-permute-start(f32[1,32,8,128]{3,2,1,0:T(8,128)S(1)} %get-tuple-element.494), channel_id=1, source_target_pairs={{0,4},{4,8},{8,12},{12,16},{16,20},{20,24},{24,28},{1,5},{5,9},{9,... | collective-permute-start | bytes 393224 | tf_op jit(solution)/shard_map/while/body/eval_jaxpr/ppermute | solution.py:25
  253.6 16.5 %collective-permute-start.2 = (f32[1,32,48,8]{2,3,1,0:T(8,128)S(1)}, f32[1,32,48,8]{2,3,1,0:T(8,128)}, u32[]{:S(2)}, u32[]{:S(2)}) collective-permute-start(f32[1,32,48,8]{2,3,1,0:T(8,128)S(1)} %copy.27), channel_id=1, source_target_pairs={{0,1},{1,2},{2,3},{4,5},{5,6},{6,7},{8,9},{9,10},{10,11},{12,13},{... | collective-permute-start | bytes 147464 | tf_op jit(solution)/shard_map/while/body/eval_jaxpr/ppermute | solution.py:25
  255.8 15.4 %collective-permute-start.3 = (f32[1,32,48,8]{2,3,1,0:T(8,128)}, f32[1,32,48,8]{2,3,1,0:T(8,128)}, u32[]{:S(2)}, u32[]{:S(2)}) collective-permute-start(f32[1,32,48,8]{2,3,1,0:T(8,128)} %copy.29), channel_id=1, source_target_pairs={{1,0},{2,1},{3,2},{5,4},{6,5},{7,6},{9,8},{10,9},{11,10},{13,12},{... | collective-permute-start | bytes 147464 | tf_op jit(solution)/shard_map/while/body/eval_jaxpr/ppermute | solution.py:27
  283.2 10.7 %collective-permute-start = (f32[1,32,8,128]{3,2,1,0:T(8,128)S(1)}, f32[1,32,8,128]{3,2,1,0:T(8,128)S(1)}, u32[]{:S(2)}, u32[]{:S(2)}) collective-permute-start(f32[1,32,8,128]{3,2,1,0:T(8,128)S(1)} %get-tuple-element.494), channel_id=1, source_target_pairs={{0,4},{4,8},{8,12},{12,16},{16,20},{20,24},{24,28},{1,5},{5,9},{9,... | collective-permute-start | bytes 393224 | tf_op jit(solution)/shard_map/while/body/eval_jaxpr/ppermute | solution.py:25
  297.7 16.5 %collective-permute-start.2 = (f32[1,32,48,8]{2,3,1,0:T(8,128)S(1)}, f32[1,32,48,8]{2,3,1,0:T(8,128)}, u32[]{:S(2)}, u32[]{:S(2)}) collective-permute-start(f32[1,32,48,8]{2,3,1,0:T(8,128)S(1)} %copy.27), channel_id=1, source_target_pairs={{0,1},{1,2},{2,3},{4,5},{5,6},{6,7},{8,9},{9,10},{10,11},{12,13},{... | collective-permute-start | bytes 147464 | tf_op jit(solution)/shard_map/while/body/eval_jaxpr/ppermute | solution.py:25
  299.9 15.4 %collective-permute-start.3 = (f32[1,32,48,8]{2,3,1,0:T(8,128)}, f32[1,32,48,8]{2,3,1,0:T(8,128)}, u32[]{:S(2)}, u32[]{:S(2)}) collective-permute-start(f32[1,32,48,8]{2,3,1,0:T(8,128)} %copy.29), channel_id=1, source_target_pairs={{1,0},{2,1},{3,2},{5,4},{6,5},{7,6},{9,8},{10,9},{11,10},{13,12},{... | collective-permute-start | bytes 147464 | tf_op jit(solution)/shard_map/while/body/eval_jaxpr/ppermute | solution.py:27
  327.3 10.7 %collective-permute-start = (f32[1,32,8,128]{3,2,1,0:T(8,128)S(1)}, f32[1,32,8,128]{3,2,1,0:T(8,128)S(1)}, u32[]{:S(2)}, u32[]{:S(2)}) collective-permute-start(f32[1,32,8,128]{3,2,1,0:T(8,128)S(1)} %get-tuple-element.494), channel_id=1, source_target_pairs={{0,4},{4,8},{8,12},{12,16},{16,20},{20,24},{24,28},{1,5},{5,9},{9,... | collective-permute-start | bytes 393224 | tf_op jit(solution)/shard_map/while/body/eval_jaxpr/ppermute | solution.py:25
  341.8 16.5 %collective-permute-start.2 = (f32[1,32,48,8]{2,3,1,0:T(8,128)S(1)}, f32[1,32,48,8]{2,3,1,0:T(8,128)}, u32[]{:S(2)}, u32[]{:S(2)}) collective-permute-start(f32[1,32,48,8]{2,3,1,0:T(8,128)S(1)} %copy.27), channel_id=1, source_target_pairs={{0,1},{1,2},{2,3},{4,5},{5,6},{6,7},{8,9},{9,10},{10,11},{12,13},{... | collective-permute-start | bytes 147464 | tf_op jit(solution)/shard_map/while/body/eval_jaxpr/ppermute | solution.py:25
  344.0 15.4 %collective-permute-start.3 = (f32[1,32,48,8]{2,3,1,0:T(8,128)}, f32[1,32,48,8]{2,3,1,0:T(8,128)}, u32[]{:S(2)}, u32[]{:S(2)}) collective-permute-start(f32[1,32,48,8]{2,3,1,0:T(8,128)} %copy.29), channel_id=1, source_target_pairs={{1,0},{2,1},{3,2},{5,4},{6,5},{7,6},{9,8},{10,9},{11,10},{13,12},{... | collective-permute-start | bytes 147464 | tf_op jit(solution)/shard_map/while/body/eval_jaxpr/ppermute | solution.py:27
  371.4 10.7 %collective-permute-start = (f32[1,32,8,128]{3,2,1,0:T(8,128)S(1)}, f32[1,32,8,128]{3,2,1,0:T(8,128)S(1)}, u32[]{:S(2)}, u32[]{:S(2)}) collective-permute-start(f32[1,32,8,128]{3,2,1,0:T(8,128)S(1)} %get-tuple-element.494), channel_id=1, source_target_pairs={{0,4},{4,8},{8,12},{12,16},{16,20},{20,24},{24,28},{1,5},{5,9},{9,... | collective-permute-start | bytes 393224 | tf_op jit(solution)/shard_map/while/body/eval_jaxpr/ppermute | solution.py:25
  385.9 16.5 %collective-permute-start.2 = (f32[1,32,48,8]{2,3,1,0:T(8,128)S(1)}, f32[1,32,48,8]{2,3,1,0:T(8,128)}, u32[]{:S(2)}, u32[]{:S(2)}) collective-permute-start(f32[1,32,48,8]{2,3,1,0:T(8,128)S(1)} %copy.27), channel_id=1, source_target_pairs={{0,1},{1,2},{2,3},{4,5},{5,6},{6,7},{8,9},{9,10},{10,11},{12,13},{... | collective-permute-start | bytes 147464 | tf_op jit(solution)/shard_map/while/body/eval_jaxpr/ppermute | solution.py:25
  388.1 15.4 %collective-permute-start.3 = (f32[1,32,48,8]{2,3,1,0:T(8,128)}, f32[1,32,48,8]{2,3,1,0:T(8,128)}, u32[]{:S(2)}, u32[]{:S(2)}) collective-permute-start(f32[1,32,48,8]{2,3,1,0:T(8,128)} %copy.29), channel_id=1, source_target_pairs={{1,0},{2,1},{3,2},{5,4},{6,5},{7,6},{9,8},{10,9},{11,10},{13,12},{... | collective-permute-start | bytes 147464 | tf_op jit(solution)/shard_map/while/body/eval_jaxpr/ppermute | solution.py:27
  415.5 10.7 %collective-permute-start = (f32[1,32,8,128]{3,2,1,0:T(8,128)S(1)}, f32[1,32,8,128]{3,2,1,0:T(8,128)S(1)}, u32[]{:S(2)}, u32[]{:S(2)}) collective-permute-start(f32[1,32,8,128]{3,2,1,0:T(8,128)S(1)} %get-tuple-element.494), channel_id=1, source_target_pairs={{0,4},{4,8},{8,12},{12,16},{16,20},{20,24},{24,28},{1,5},{5,9},{9,... | collective-permute-start | bytes 393224 | tf_op jit(solution)/shard_map/while/body/eval_jaxpr/ppermute | solution.py:25
  430.0 16.5 %collective-permute-start.2 = (f32[1,32,48,8]{2,3,1,0:T(8,128)S(1)}, f32[1,32,48,8]{2,3,1,0:T(8,128)}, u32[]{:S(2)}, u32[]{:S(2)}) collective-permute-start(f32[1,32,48,8]{2,3,1,0:T(8,128)S(1)} %copy.27), channel_id=1, source_target_pairs={{0,1},{1,2},{2,3},{4,5},{5,6},{6,7},{8,9},{9,10},{10,11},{12,13},{... | collective-permute-start | bytes 147464 | tf_op jit(solution)/shard_map/while/body/eval_jaxpr/ppermute | solution.py:25
  432.2 15.4 %collective-permute-start.3 = (f32[1,32,48,8]{2,3,1,0:T(8,128)}, f32[1,32,48,8]{2,3,1,0:T(8,128)}, u32[]{:S(2)}, u32[]{:S(2)}) collective-permute-start(f32[1,32,48,8]{2,3,1,0:T(8,128)} %copy.29), channel_id=1, source_target_pairs={{1,0},{2,1},{3,2},{5,4},{6,5},{7,6},{9,8},{10,9},{11,10},{13,12},{... | collective-permute-start | bytes 147464 | tf_op jit(solution)/shard_map/while/body/eval_jaxpr/ppermute | solution.py:27
  459.6 10.7 %collective-permute-start = (f32[1,32,8,128]{3,2,1,0:T(8,128)S(1)}, f32[1,32,8,128]{3,2,1,0:T(8,128)S(1)}, u32[]{:S(2)}, u32[]{:S(2)}) collective-permute-start(f32[1,32,8,128]{3,2,1,0:T(8,128)S(1)} %get-tuple-element.494), channel_id=1, source_target_pairs={{0,4},{4,8},{8,12},{12,16},{16,20},{20,24},{24,28},{1,5},{5,9},{9,... | collective-permute-start | bytes 393224 | tf_op jit(solution)/shard_map/while/body/eval_jaxpr/ppermute | solution.py:25
  474.1 16.5 %collective-permute-start.2 = (f32[1,32,48,8]{2,3,1,0:T(8,128)S(1)}, f32[1,32,48,8]{2,3,1,0:T(8,128)}, u32[]{:S(2)}, u32[]{:S(2)}) collective-permute-start(f32[1,32,48,8]{2,3,1,0:T(8,128)S(1)} %copy.27), channel_id=1, source_target_pairs={{0,1},{1,2},{2,3},{4,5},{5,6},{6,7},{8,9},{9,10},{10,11},{12,13},{... | collective-permute-start | bytes 147464 | tf_op jit(solution)/shard_map/while/body/eval_jaxpr/ppermute | solution.py:25
  476.3 15.4 %collective-permute-start.3 = (f32[1,32,48,8]{2,3,1,0:T(8,128)}, f32[1,32,48,8]{2,3,1,0:T(8,128)}, u32[]{:S(2)}, u32[]{:S(2)}) collective-permute-start(f32[1,32,48,8]{2,3,1,0:T(8,128)} %copy.29), channel_id=1, source_target_pairs={{1,0},{2,1},{3,2},{5,4},{6,5},{7,6},{9,8},{10,9},{11,10},{13,12},{... | collective-permute-start | bytes 147464 | tf_op jit(solution)/shard_map/while/body/eval_jaxpr/ppermute | solution.py:27
  (76 other events, 504.0 us)
Sparse Core Ops, SparseCore 0:
  506.1 91.2 reduce-scatter.1
where the time goes:
time: 609 us; the launch traced here: 606 us
  starting transfers between devices  158 us (26%)
  other arithmetic  145 us (24%)
  waiting for transfers between devices  111 us (18%)
  local copies, waits for them, and re-layouts  107 us (18%)
  blocking collectives  50.9 us (8%)
  loops' own time  18.4 us (3%)
  between operations  15.4 us (3%)
    ppermute x20, starting transfers between devices, with_halo(): lax.ppermute(tail, axis, [(i, (i + 1) % count) for i in range(ends)])  93 us
    reduce_scatter x1, waiting for transfers between devices, shards(): lax.psum_scatter(weighted, 'shot', scatter_dimension=0, tiled=True)  91.4 us
    add x10, other arithmetic, one_step(): updated = 2.0 * current - previous + velocity * laplace(padded)  70.6 us
    ppermute x20, starting transfers between devices, with_halo(): lax.ppermute(head, axis, [((i + 1) % count, i) for i in range(ends)])  64.8 us
    scatter-add x10, other arithmetic, inject(): surface = jnp.zeros((shots_here * span_x * span_y,), jnp.float32).at[flat...  60.6 us
    all_gather x1, blocking collectives, shards(): velocity = lax.all_gather(model, 'shot', axis=0, tiled=True)  50.9 us
    while x160, local copies, waits for them, and re-layouts  24.8 us
    slice x30, local copies, waits for them, and re-layouts, with_halo(): head = lax.slice_in_dim(cells, 0, width, axis=dim)  20.9 us
  transfers between devices with their start and end apart: 41, of which 11 were waited for; matrix products, arithmetic and copies ran while one was open for 17% of the time, Pallas kernels for 0%

commit v1 on v0

v1 whole, which is shorter than its diff:
```python
import math

import jax
import jax.numpy as jnp
from jax import lax
from jax.experimental import pallas as pl
from jax.experimental.pallas import tpu as pltpu
from jax.sharding import PartitionSpec as P

STEPS = 10
REACH = 8
SPLIT = 4

rec_depth = 2
src_depth = 3.0
mute_radius = 10.0
step_size = 0.01

MESH = pl.DeviceIdType.MESH
F32 = jnp.float32
BF16 = jnp.bfloat16


def coefficients():
    weights_table = []
    for offset in range(1, 9):
        weights_table.append(
            2.0
            * (-1.0) ** (offset + 1)
            * math.factorial(8) ** 2
            / (offset * offset * math.factorial(8 - offset) * math.factorial(8 + offset))
        )
    centre = -2.0 * sum(weights_table)
    return (centre, weights_table)


def halves(value):
    high = value.astype(BF16)
    low = (value - high.astype(F32)).astype(BF16)
    return high, low


def kernel(
    prior_ref,
    now_ref,
    fwd_ref,
    res_ref,
    rx_ref,
    ry_ref,
    sx_ref,
    sy_ref,
    slot_ref,
    model_ref,
    out_ref,
    grad_ref,
    upd_ref,
    field,
    speed,
    saved,
    image,
    surface,
    ylap,
    band,
    xin,
    yout,
    yin,
    pass_in,
    pass_out,
    near_in,
    part,
    last_in,
    load_sem,
    x_send,
    x_recv,
    y_send,
    y_recv,
    gz_send,
    gz_recv,
    gx_send,
    gx_recv,
    gr_send,
    gr_recv,
    ra_send,
    ra_recv,
    rb_send,
    rb_recv,
    rd_send,
    rd_recv,
):
    centre, weights = coefficients()
    depth, span_x, span_y = speed.shape
    layers = depth // SPLIT
    tiles = span_x // 8
    shot, tx, ty = lax.axis_index("shot"), lax.axis_index("tx"), lax.axis_index("ty")
    zl, col = lax.rem(shot, 4), lax.div(shot, 4)
    right, left = lax.rem(col + 1, 4), lax.rem(col + 3, 4)
    opposite = lax.rem(col + 2, 4)
    to_right = {"shot": right * 4 + zl}
    to_left = {"shot": left * 4 + zl}
    x_ends = ((tx > 0, {"tx": tx - 1}), (tx < lax.axis_size("tx") - 1, {"tx": tx + 1}))
    y_ends = ((ty > 0, {"ty": ty - 1}), (ty < lax.axis_size("ty") - 1, {"ty": ty + 1}))

    def zl_peer(distance):
        return lax.rem(zl + distance, 4)

    loads = [
        pltpu.make_async_copy(
            now_ref.at[0], field.at[0, pl.ds(8, depth), pl.ds(8, span_x), :], load_sem.at[0]
        ),
        pltpu.make_async_copy(
            prior_ref.at[0], field.at[1, pl.ds(8, depth), pl.ds(8, span_x), :], load_sem.at[1]
        ),
        pltpu.make_async_copy(fwd_ref.at[0], saved, load_sem.at[2]),
        pltpu.make_async_copy(model_ref, speed.at[pl.ds(2 * shot, 2)], load_sem.at[3]),
    ]
    for load in loads:
        load.start()

    xin[...] = jnp.zeros_like(xin)
    yin[...] = jnp.zeros_like(yin)

    barrier = pltpu.get_barrier_semaphore()
    for present, peer in x_ends + y_ends:

        @pl.when(present)
        def _(peer=peer):
            pl.semaphore_signal(barrier, inc=1, device_id=peer, device_id_type=MESH)

    for distance in (1, 2, 3):
        pl.semaphore_signal(
            barrier, inc=1, device_id={"shot": col * 4 + zl_peer(distance)}, device_id_type=MESH
        )
    for peer in (to_right, to_left):
        pl.semaphore_signal(barrier, inc=1, device_id=peer, device_id_type=MESH)
    for par in range(2):
        field[par, pl.ds(0, 8)] = jnp.zeros((8, span_x + 16, span_y), F32)
        field[par, pl.ds(depth + 8, 8)] = jnp.zeros((8, span_x + 16, span_y), F32)
        field[par, pl.ds(8, depth), pl.ds(0, 8)] = jnp.zeros((depth, 8, span_y), F32)
        field[par, pl.ds(8, depth), pl.ds(span_x + 8, 8)] = jnp.zeros((depth, 8, span_y), F32)
    neighbours = 5
    for present, _ in x_ends + y_ends:
        neighbours = neighbours + present.astype(jnp.int32)
    pl.semaphore_wait(barrier, neighbours)

    def gather_z(distance):
        return pltpu.make_async_remote_copy(
            src_ref=model_ref,
            dst_ref=speed.at[pl.ds(2 * shot, 2)],
            send_sem=gz_send.at[distance - 1],
            recv_sem=gz_recv.at[distance - 1],
            device_id={"shot": col * 4 + zl_peer(distance)},
            device_id_type=MESH,
        )

    def gather_x(block, side):
        where = pl.ds(2 * (col * 4 + zl_peer(4 - block)), 2)
        return pltpu.make_async_remote_copy(
            src_ref=model_ref if block == 0 else speed.at[where],
            dst_ref=speed.at[where],
            send_sem=gx_send.at[block, side],
            recv_sem=gx_recv.at[block, side],
            device_id=to_right if side else to_left,
            device_id_type=MESH,
        )

    def gather_relay(block):
        origin = left if block < 2 else right
        where = pl.ds(2 * (origin * 4 + zl_peer(4 - block)), 2)
        return pltpu.make_async_remote_copy(
            src_ref=speed.at[where],
            dst_ref=speed.at[where],
            send_sem=gr_send.at[block],
            recv_sem=gr_recv.at[block],
            device_id=to_right if block < 2 else to_left,
            device_id_type=MESH,
        )

    def x_copy(par, c, side, source):
        zs = pl.ds(layers * c, layers)
        if source is None:
            src = field.at[par, pl.ds(8 + layers * c, layers), pl.ds(8 + (span_x - 8) * side, 8), :]
        else:
            src = source.at[0, zs, pl.ds((span_x - 8) * side, 8), :]
        return pltpu.make_async_remote_copy(
            src_ref=src,
            dst_ref=xin.at[par, c, 1 - side, :, pl.ds(8 * (1 - side), 8), :],
            send_sem=x_send.at[par, c, side],
            recv_sem=x_recv.at[par, c, 1 - side],
            device_id=x_ends[side][1],
            device_id_type=MESH,
        )

    def y_copy(par, c, side):
        return pltpu.make_async_remote_copy(
            src_ref=yout.at[par, c],
            dst_ref=yin.at[par, c, 1 - side],
            send_sem=y_send.at[par, c, side],
            recv_sem=y_recv.at[par, c, 1 - side],
            device_id=y_ends[side][1],
            device_id_type=MESH,
        )

    def each_end(ends, action):
        for side in range(2):

            @pl.when(ends[side][0])
            def _(side=side):
                action(side)

    for distance in (1, 2, 3):
        gather_z(distance).start()
    for side in range(2):
        gather_x(0, side).start()
    for c in range(SPLIT):
        each_end(x_ends, lambda side, c=c: x_copy(0, c, side, now_ref).start())

    lane = lax.broadcasted_iota(jnp.int32, (8, span_y), 1)
    group = lax.div(lane, 16)
    from_left = lax.rem(lane, 16) < 8

    def pack_y(par, c):
        for t in range(tiles):
            packed = jnp.zeros((8, span_y), F32)
            for j in range(layers):
                value = field[par, 8 + layers * c + j, pl.ds(8 + 8 * t, 8), :]
                packed = jnp.where(group == j, pltpu.roll(value, (16 * j + 8) % span_y, 1), packed)
            yout[par, c, t] = packed

    loads[0].wait()
    for c in range(SPLIT):
        pack_y(0, c)
        each_end(y_ends, lambda side, c=c: y_copy(0, c, side).start())

    row = lax.broadcasted_iota(jnp.int32, (span_y, span_y), 0)
    column = lax.broadcasted_iota(jnp.int32, (span_y, span_y), 1)
    away = jnp.abs(row - column)
    inner = lax.rem(row, 16)
    halo_away = jnp.where(inner < 8, column + 8 - inner, span_y - 8 + inner - column)
    own = jnp.zeros((span_y, span_y), F32)
    edge = jnp.zeros((span_y, span_y), F32)
    for k in range(1, 9):
        own = jnp.where(away == k, F32(weights[k - 1]), own)
        edge = jnp.where(halo_away == k, F32(weights[k - 1]), edge)
    for i, matrix in enumerate((own, edge)):
        high, low = halves(matrix)
        band[pl.ds(256 * i, 128), pl.ds(0, 128)] = high
        band[pl.ds(256 * i, 128), pl.ds(128, 128)] = low
        band[pl.ds(256 * i + 128, 128), pl.ds(0, 128)] = high
        band[pl.ds(256 * i + 128, 128), pl.ds(128, 128)] = jnp.zeros((128, 128), BF16)

    for block in (1, 2, 3):
        gather_z(block).wait_recv()
        for side in range(2):
            gather_x(block, side).start()

    count = rx_ref.shape[1]
    local_x = rx_ref[...] - tx * span_x
    local_y = ry_ref[...] - ty * span_y
    at_x = local_x == lax.broadcasted_iota(jnp.int32, (span_x, count), 0)
    at_y = (local_y == lax.broadcasted_iota(jnp.int32, (span_y, count), 0)).astype(F32).astype(BF16)

    def spread(moment, carry):
        traces = jnp.where(at_x, res_ref[0, pl.ds(moment, 1), :], 0.0)
        high = traces.astype(BF16)
        rest = traces - high.astype(F32)
        mid = rest.astype(BF16)
        low = (rest - mid.astype(F32)).astype(BF16)
        total = jnp.zeros((span_x, span_y), F32)
        for term in (low, mid, high):
            total = total + lax.dot_general(
                term, at_y, (((1,), (1,)), ((), ())), preferred_element_type=F32
            )
        surface[moment] = total
        return carry

    lax.fori_loop(0, STEPS, spread, 0)

    for block in range(4):
        gather_x(block, 1).wait_recv()
        if block < 2:
            gather_relay(block).start()
        gather_x(block, 0).wait_recv()
        if block >= 2:
            gather_relay(block).start()
    for block in range(4):
        gather_relay(block).wait_recv()
    for load in loads[1:]:
        load.wait()

    def zero_image(z, carry):
        image[z] = jnp.zeros((span_x, span_y), F32)
        return carry

    lax.fori_loop(0, depth, zero_image, 0)

    def before(n, c):
        par = lax.rem(n, 2)

        @pl.when(n > 0)
        def _():
            each_end(x_ends, lambda side: x_copy(1 - par, c, side, None).wait_send())
            each_end(y_ends, lambda side: y_copy(1 - par, c, side).wait_send())

        each_end(y_ends, lambda side: y_copy(par, c, 1 - side).wait_recv())
        base = layers * c
        value = field[par, pl.ds(8 + base, layers), pl.ds(8, span_x), :].reshape(
            layers * span_x, span_y
        )
        high, low = halves(value)
        halo = []
        for t in range(tiles):
            halo.append(jnp.where(from_left, yin[par, c, 0, t], yin[par, c, 1, t]))
        halo = jnp.concatenate(halo, axis=0)
        groups = lax.div(lax.broadcasted_iota(jnp.int32, (span_x, span_y), 1), 16)
        halo = jnp.concatenate([jnp.where(groups == j, halo, 0.0) for j in range(layers)], axis=0)
        halo_high, halo_low = halves(halo)
        sides = jnp.dot(
            jnp.concatenate([high, low, halo_high, halo_low], axis=1),
            band[...],
            preferred_element_type=F32,
        )
        ylap[...] = (sides[:, :span_y] + sides[:, span_y:]).reshape(layers, span_x, span_y)
        for t in range(tiles):
            rows = pl.ds(8 + 8 * t, 8)
            plane = [field[par, base + i, rows, :] for i in range(layers + 16)]
            for j in range(layers):
                total = ylap[j, pl.ds(8 * t, 8), :]
                for k in range(1, 9):
                    pairs = (plane[8 + j + k] + plane[8 + j - k]) + (
                        field[par, 8 + base + j, pl.ds(8 + 8 * t + k, 8), :]
                        + field[par, 8 + base + j, pl.ds(8 + 8 * t - k, 8), :]
                    )
                    total = total + F32(weights[k - 1]) * pairs
                here = plane[8 + j]
                total = total + F32(3.0 * centre) * here
                field[1 - par, 8 + base + j, rows, :] = (
                    2.0 * here
                    - field[1 - par, 8 + base + j, rows, :]
                    + speed[base + j, pl.ds(8 * t, 8), :] * total
                )

        @pl.when(c == 0)
        def _():
            at = (1 - par, 8 + rec_depth, pl.ds(8, span_x))
            field[at] = field[at] + surface[STEPS - 1 - n]

    def after(n, c):
        par = lax.rem(n, 2)
        base = layers * c
        each_end(x_ends, lambda side: x_copy(par, c, 1 - side, None).wait_recv())
        for side in range(2):
            t = (tiles - 1) * side
            for j in range(layers):
                total = jnp.zeros((8, span_y), F32)
                for k in range(1, 9):
                    start = k if side else 8 - k
                    total = total + F32(weights[k - 1]) * xin[par, c, side, j, pl.ds(start, 8), :]
                rows = pl.ds(8 + 8 * t, 8)
                field[1 - par, 8 + base + j, rows, :] = (
                    field[1 - par, 8 + base + j, rows, :]
                    + speed[base + j, pl.ds(8 * t, 8), :] * total
                )

    before(0, 0)

    def slot(s, carry):
        n, c = lax.div(s, SPLIT), lax.rem(s, SPLIT)
        nxt = 1 - lax.rem(n, 2)
        after(n, c)

        @pl.when(n < STEPS - 1)
        def _():
            each_end(x_ends, lambda side: x_copy(nxt, c, side, None).start())
            pack_y(nxt, c)
            each_end(y_ends, lambda side: y_copy(nxt, c, side).start())

        which = slot_ref[STEPS - 1 - n]
        zs = pl.ds(layers * c, layers)
        image[zs] = image[zs] + saved[which, zs] * (
            field[nxt, pl.ds(8 + layers * c, layers), pl.ds(8, span_x), :]
        )

        @pl.when(s + 1 < STEPS * SPLIT)
        def _():
            before(lax.div(s + 1, SPLIT), lax.rem(s + 1, SPLIT))

        return carry

    lax.fori_loop(0, STEPS * SPLIT, slot, 0)
    end = STEPS % 2
    result = pltpu.make_async_copy(
        field.at[end, pl.ds(8, depth), pl.ds(8, span_x), :], out_ref.at[0], load_sem.at[0]
    )
    result.start()

    sx = sx_ref[0].astype(F32)
    sy = sy_ref[0].astype(F32)
    cell_x = (tx * span_x + lax.broadcasted_iota(jnp.int32, (span_x, span_y), 0)).astype(F32) - sx
    cell_y = (ty * span_y + lax.broadcasted_iota(jnp.int32, (span_x, span_y), 1)).astype(F32) - sy
    flat = cell_x * cell_x + cell_y * cell_y

    def mute(z, carry):
        gap = z.astype(F32) - src_depth
        image[z] = image[z] * (1.0 - jnp.exp(-(gap * gap + flat) / (mute_radius * mute_radius)))
        return carry

    lax.fori_loop(0, depth, mute, 0)

    def piece(column_at, q):
        return pl.ds(8 * column_at + 2 * q, 2)

    def sum_far(q):
        return pltpu.make_async_remote_copy(
            src_ref=image.at[piece(opposite, q)],
            dst_ref=pass_in.at[q],
            send_sem=ra_send.at[q],
            recv_sem=ra_recv.at[q],
            device_id=to_right if q < 2 else to_left,
            device_id_type=MESH,
        )

    def sum_near(q, side):
        combined = (q < 2) == (side == 1)
        return pltpu.make_async_remote_copy(
            src_ref=pass_out.at[q] if combined else image.at[piece(right if side else left, q)],
            dst_ref=near_in.at[1 - side, q],
            send_sem=rb_send.at[q, side],
            recv_sem=rb_recv.at[q, 1 - side],
            device_id=to_right if side else to_left,
            device_id_type=MESH,
        )

    def sum_depth(distance):
        return pltpu.make_async_remote_copy(
            src_ref=part.at[zl_peer(distance)],
            dst_ref=last_in.at[distance - 1],
            send_sem=rd_send.at[distance - 1],
            recv_sem=rd_recv.at[distance - 1],
            device_id={"shot": col * 4 + zl_peer(distance)},
            device_id_type=MESH,
        )

    for q in range(4):
        sum_far(q).start()
    for q in range(4):
        sum_near(q, 0 if q < 2 else 1).start()
    for q in range(4):
        sum_far(q).wait_recv()
        pass_out[q] = pass_in[q] + image[piece(right if q < 2 else left, q)]
        sum_near(q, 1 if q < 2 else 0).start()
    for q in range(4):
        sum_near(q, 0).wait_recv()
        sum_near(q, 1).wait_recv()
        part[q] = image[piece(col, q)] + near_in[0, q] + near_in[1, q]
    for distance in (1, 2, 3):
        sum_depth(distance).start()
    total = part[zl]
    for distance in (1, 2, 3):
        sum_depth(distance).wait_recv()
        total = total + last_in[distance - 1]
    gradient = total * F32(1.0 / math.sqrt(lax.axis_size("shot") * STEPS))
    grad_ref[...] = gradient
    upd_ref[...] = model_ref[...] - step_size * gradient

    last = (STEPS - 1) % 2
    for c in range(SPLIT):
        each_end(x_ends, lambda side, c=c: x_copy(last, c, side, None).wait_send())
        each_end(y_ends, lambda side, c=c: y_copy(last, c, side).wait_send())
    for distance in (1, 2, 3):
        gather_z(distance).wait_send()
        sum_depth(distance).wait_send()
    for q in range(4):
        gather_relay(q).wait_send()
        sum_far(q).wait_send()
        for side in range(2):
            gather_x(q, side).wait_send()
            sum_near(q, side).wait_send()
    result.wait()


def shards(
    adjoint_prior,
    adjoint_now,
    forward_saved,
    residuals,
    receiver_x,
    receiver_y,
    source_x,
    source_y,
    saved_slot,
    model,
):
    _, depth, span_x, span_y = adjoint_now.shape
    layers = depth // SPLIT
    tiles = span_x // 8
    anywhere = pl.BlockSpec(memory_space=pl.ANY)
    vmem = pl.BlockSpec(memory_space=pltpu.VMEM)
    smem = pl.BlockSpec(memory_space=pltpu.SMEM)
    dma = pltpu.SemaphoreType.DMA
    return pl.pallas_call(
        kernel,
        out_shape=(
            jax.ShapeDtypeStruct(adjoint_now.shape, F32),
            jax.ShapeDtypeStruct(model.shape, F32),
            jax.ShapeDtypeStruct(model.shape, F32),
        ),
        in_specs=[anywhere, anywhere, anywhere, vmem, vmem, vmem, smem, smem, smem, vmem],
        out_specs=(anywhere, vmem, vmem),
        scratch_shapes=[
            pltpu.VMEM((2, depth + 16, span_x + 16, span_y), F32),
            pltpu.VMEM((depth, span_x, span_y), F32),
            pltpu.VMEM((2, depth, span_x, span_y), F32),
            pltpu.VMEM((depth, span_x, span_y), F32),
            pltpu.VMEM((STEPS, span_x, span_y), F32),
            pltpu.VMEM((layers, span_x, span_y), F32),
            pltpu.VMEM((512, 256), BF16),
            pltpu.VMEM((2, SPLIT, 2, layers, 16, span_y), F32),
            pltpu.VMEM((2, SPLIT, tiles, 8, span_y), F32),
            pltpu.VMEM((2, SPLIT, 2, tiles, 8, span_y), F32),
            pltpu.VMEM((4, 2, span_x, span_y), F32),
            pltpu.VMEM((4, 2, span_x, span_y), F32),
            pltpu.VMEM((2, 4, 2, span_x, span_y), F32),
            pltpu.VMEM((4, 2, span_x, span_y), F32),
            pltpu.VMEM((3, 2, span_x, span_y), F32),
            dma((4,)),
            dma((2, SPLIT, 2)),
            dma((2, SPLIT, 2)),
            dma((2, SPLIT, 2)),
            dma((2, SPLIT, 2)),
            dma((3,)),
            dma((3,)),
            dma((4, 2)),
            dma((4, 2)),
            dma((4,)),
            dma((4,)),
            dma((4,)),
            dma((4,)),
            dma((4, 2)),
            dma((4, 2)),
            dma((3,)),
            dma((3,)),
        ],
        compiler_params=pltpu.CompilerParams(
            collective_id=0, has_side_effects=True, vmem_limit_bytes=40 * 1024 * 1024
        ),
    )(
        adjoint_prior,
        adjoint_now,
        forward_saved,
        residuals,
        receiver_x,
        receiver_y,
        source_x,
        source_y,
        saved_slot,
        model,
    )


def solution(mesh):
    return jax.shard_map(
        shards,
        mesh=mesh,
        in_specs=(
            P("shot", None, "tx", "ty"),
            P("shot", None, "tx", "ty"),
            P("shot", None, None, "tx", "ty"),
            P("shot", None, None),
            P("shot", None),
            P("shot", None),
            P("shot"),
            P("shot"),
            P(),
            P("shot", "tx", "ty"),
        ),
        out_specs=(P("shot", None, "tx", "ty"), P("shot", "tx", "ty"), P("shot", "tx", "ty")),
        check_vma=False,
    )
```

time: 609 us -> 111 us (0.18)
  the two profiles are of different devices: /device:TPU:24 before, /device:TPU:1 now
where the time goes in v1:
time: 111 us; the launch traced here: 110 us
  Pallas kernels  102 us (92%)
  local copies, waits for them, and re-layouts  6.16 us (6%)
  between operations  2.01 us (2%)
    pallas_call x1, Pallas kernels, shards(): pl.pallas_call(kernel, out_shape=(jax.ShapeDtypeStruct(adjoint_now.shape,...  102 us
    unnamed x18, local copies, waits for them, and re-layouts  6.16 us

profile of v1, /device:TPU:1, one launch (start us, length us, event | category | flops | bytes accessed | tf_op | source)
XLA Modules:
  0.0 110.5 jit_solution(15771199916772977461)
XLA Ops:
  1.9 0.0 copy-start.3
  1.9 0.0 copy-start.4
  1.9 0.0 copy-start.5
  2.0 0.0 copy-start.6
  2.0 0.8 copy.13.res_ref
  2.8 0.0 copy-done.3
  2.8 0.0 copy-done.4
  2.8 0.0 copy-done.5
  2.8 0.0 copy-done.6
  2.8 0.0 copy-start
  2.8 1.2 %copy-done = f32[1,2,32,32,128]{4,3,2,1,0:T(8,128)S(1)} copy-done((f32[1,2,32,32,128]{4,3,2,1,0:T(8,128)S(1)}, f32[1,2,32,32,128]{4,3,2,1,0:T(8,128)}, u32[]{:S(2)}) %copy-start) | copy-done | bytes 1048600
  4.0 0.0 copy-start.1
  4.1 1.0 copy-done.1
  5.1 0.0 copy-start.2
  5.1 1.0 copy-done.2
  6.1 102.3 %shard_map.121 = (f32[1,32,32,128]{3,2,1,0:T(8,128)S(1)}, f32[2,32,128]{2,1,0:T(8,128)S(1)}, f32[2,32,128]{2,1,0:T(8,128)S(1)}) custom-call(f32[1,32,32,128]{3,2,1,0:T(8,128)S(1)} %copy-done.1, f32[1,32,32,128]{3,2,1,0:T(8,128)S(1)} %copy-done.2, f32[1,2,32,32,128]{4,3,2,1,0:T(8,128)S(1)} %copy-done, f32[1,10,1024]{2,1,0:T(8,128)S(1)} %copy.13.res_ref, ...), custom_call_target="tpu_custom_call" | custom-call | tf_op jit(solution)/shard_map/pallas_call | solution.py:500
  108.5 0.8 copy.19
  109.2 0.6 copy.20
  109.9 0.6 copy.21
Async XLA Ops:
  1.9 0.9 copy-start.3
  1.9 0.9 copy-start.4
  1.9 0.9 copy-start.5
  2.0 0.9 copy-start.6
  2.8 1.2 %copy-start = (f32[1,2,32,32,128]{4,3,2,1,0:T(8,128)S(1)}, f32[1,2,32,32,128]{4,3,2,1,0:T(8,128)}, u32[]{:S(2)}) copy-start(f32[1,2,32,32,128]{4,3,2,1,0:T(8,128)} %fwd_ref.1) | copy-start | bytes 3145732
  4.0 1.0 copy-start.1
  5.1 1.0 copy-start.2

commit v2 on v1

--- a/solution.py
+++ b/solution.py
@@ -52,8 +52,7 @@
     slot_ref,
     model_ref,
     out_ref,
-    grad_ref,
-    upd_ref,
+    sum_ref,
     field,
     speed,
     saved,
@@ -140,7 +139,6 @@
     neighbours = 5
     for present, _ in x_ends + y_ends:
         neighbours = neighbours + present.astype(jnp.int32)
-    pl.semaphore_wait(barrier, neighbours)
 
     def gather_z(distance):
         return pltpu.make_async_remote_copy(
@@ -206,13 +204,6 @@
             @pl.when(ends[side][0])
             def _(side=side):
                 action(side)
-
-    for distance in (1, 2, 3):
-        gather_z(distance).start()
-    for side in range(2):
-        gather_x(0, side).start()
-    for c in range(SPLIT):
-        each_end(x_ends, lambda side, c=c: x_copy(0, c, side, now_ref).start())
 
     lane = lax.broadcasted_iota(jnp.int32, (8, span_y), 1)
     group = lax.div(lane, 16)
@@ -229,6 +220,14 @@
     loads[0].wait()
     for c in range(SPLIT):
         pack_y(0, c)
+    pl.semaphore_wait(barrier, neighbours)
+    for distance in (1, 2, 3):
+        gather_z(distance).start()
+    for side in range(2):
+        gather_x(0, side).start()
+    for c in range(SPLIT):
+        each_end(x_ends, lambda side, c=c: x_copy(0, c, side, now_ref).start())
+    for c in range(SPLIT):
         each_end(y_ends, lambda side, c=c: y_copy(0, c, side).start())
 
     row = lax.broadcasted_iota(jnp.int32, (span_y, span_y), 0)
@@ -248,11 +247,6 @@
         band[pl.ds(256 * i + 128, 128), pl.ds(0, 128)] = high
         band[pl.ds(256 * i + 128, 128), pl.ds(128, 128)] = jnp.zeros((128, 128), BF16)
 
-    for block in (1, 2, 3):
-        gather_z(block).wait_recv()
-        for side in range(2):
-            gather_x(block, side).start()
-
     count = rx_ref.shape[1]
     local_x = rx_ref[...] - tx * span_x
     local_y = ry_ref[...] - ty * span_y
@@ -260,7 +254,7 @@
     at_y = (local_y == lax.broadcasted_iota(jnp.int32, (span_y, count), 0)).astype(F32).astype(BF16)
 
     def spread(moment, carry):
-        traces = jnp.where(at_x, res_ref[0, pl.ds(moment, 1), :], 0.0)
+        traces = jnp.where(at_x, res_ref[moment], 0.0)
         high = traces.astype(BF16)
         rest = traces - high.astype(F32)
         mid = rest.astype(BF16)
@@ -275,33 +269,13 @@
 
     lax.fori_loop(0, STEPS, spread, 0)
 
-    for block in range(4):
-        gather_x(block, 1).wait_recv()
-        if block < 2:
-            gather_relay(block).start()
-        gather_x(block, 0).wait_recv()
-        if block >= 2:
-            gather_relay(block).start()
-    for block in range(4):
-        gather_relay(block).wait_recv()
-    for load in loads[1:]:
-        load.wait()
-
-    def zero_image(z, carry):
-        image[z] = jnp.zeros((span_x, span_y), F32)
-        return carry
-
-    lax.fori_loop(0, depth, zero_image, 0)
-
-    def before(n, c):
-        par = lax.rem(n, 2)
-
-        @pl.when(n > 0)
-        def _():
-            each_end(x_ends, lambda side: x_copy(1 - par, c, side, None).wait_send())
-            each_end(y_ends, lambda side: y_copy(1 - par, c, side).wait_send())
-
-        each_end(y_ends, lambda side: y_copy(par, c, 1 - side).wait_recv())
+    def chunk_at(place):
+        return lax.rem(col + (2, 1, 3, 0)[place], SPLIT)
+
+    def chunk_of(place):
+        return lax.rem(col + 2 + 3 * place + 3 * lax.div(place * (place - 1), 2), SPLIT)
+
+    def stencil(par, c, store):
         base = layers * c
         value = field[par, pl.ds(8 + base, layers), pl.ds(8, span_x), :].reshape(
             layers * span_x, span_y
@@ -323,6 +297,7 @@
         for t in range(tiles):
             rows = pl.ds(8 + 8 * t, 8)
             plane = [field[par, base + i, rows, :] for i in range(layers + 16)]
+            made = []
             for j in range(layers):
                 total = ylap[j, pl.ds(8 * t, 8), :]
                 for k in range(1, 9):
@@ -332,17 +307,53 @@
                     )
                     total = total + F32(weights[k - 1]) * pairs
                 here = plane[8 + j]
-                total = total + F32(3.0 * centre) * here
-                field[1 - par, 8 + base + j, rows, :] = (
-                    2.0 * here
-                    - field[1 - par, 8 + base + j, rows, :]
-                    + speed[base + j, pl.ds(8 * t, 8), :] * total
-                )
-
+                made.append((here, total + F32(3.0 * centre) * here))
+            store(t, made)
+
+    def add_receivers(n, c):
         @pl.when(c == 0)
         def _():
-            at = (1 - par, 8 + rec_depth, pl.ds(8, span_x))
+            at = (1 - lax.rem(n, 2), 8 + rec_depth, pl.ds(8, span_x))
             field[at] = field[at] + surface[STEPS - 1 - n]
+
+    def before(n, c):
+        par = lax.rem(n, 2)
+        each_end(x_ends, lambda side: x_copy(1 - par, c, side, None).wait_send())
+        each_end(y_ends, lambda side: y_copy(1 - par, c, side).wait_send())
+        each_end(y_ends, lambda side: y_copy(par, c, 1 - side).wait_recv())
+        base = layers * c
+
+        def store(t, made):
+            rows = pl.ds(8 + 8 * t, 8)
+            new = [
+                2.0 * here
+                - field[1 - par, 8 + base + j, rows, :]
+                + speed[base + j, pl.ds(8 * t, 8), :] * total
+                for j, (here, total) in enumerate(made)
+            ]
+            for j in range(layers):
+                field[1 - par, 8 + base + j, rows, :] = new[j]
+
+        stencil(par, c, store)
+        add_receivers(n, c)
+
+    def before_first(c):
+        each_end(y_ends, lambda side: y_copy(0, c, 1 - side).wait_recv())
+        base = layers * c
+
+        def store(t, made):
+            for j in range(layers):
+                image[base + j, pl.ds(8 * t, 8), :] = made[j][1]
+
+        stencil(0, c, store)
+
+    def finish_first(c):
+        zs = pl.ds(layers * c, layers)
+        inside = (pl.ds(8 + layers * c, layers), pl.ds(8, span_x))
+        field[(1,) + inside] = (
+            2.0 * field[(0,) + inside] - field[(1,) + inside] + speed[zs] * image[zs]
+        )
+        add_receivers(0, c)
 
     def after(n, c):
         par = lax.rem(n, 2)
@@ -350,48 +361,71 @@
         each_end(x_ends, lambda side: x_copy(par, c, 1 - side, None).wait_recv())
         for side in range(2):
             t = (tiles - 1) * side
+            rows = pl.ds(8 + 8 * t, 8)
+            new = []
             for j in range(layers):
                 total = jnp.zeros((8, span_y), F32)
                 for k in range(1, 9):
                     start = k if side else 8 - k
                     total = total + F32(weights[k - 1]) * xin[par, c, side, j, pl.ds(start, 8), :]
-                rows = pl.ds(8 + 8 * t, 8)
-                field[1 - par, 8 + base + j, rows, :] = (
+                new.append(
                     field[1 - par, 8 + base + j, rows, :]
                     + speed[base + j, pl.ds(8 * t, 8), :] * total
                 )
-
-    before(0, 0)
+            for j in range(layers):
+                field[1 - par, 8 + base + j, rows, :] = new[j]
+
+    def send(n, c):
+        nxt = 1 - lax.rem(n, 2)
+        each_end(x_ends, lambda side: x_copy(nxt, c, side, None).start())
+        pack_y(nxt, c)
+        each_end(y_ends, lambda side: y_copy(nxt, c, side).start())
+
+    def imaged(n, c):
+        zs = pl.ds(layers * c, layers)
+        inside = (1 - lax.rem(n, 2), pl.ds(8 + layers * c, layers), pl.ds(8, span_x))
+        return saved[slot_ref[STEPS - 1 - n], zs] * field[inside]
+
+    for block in (1, 2, 3):
+        gather_z(block).wait_recv()
+        for side in range(2):
+            gather_x(block, side).start()
+    for place in (0, 1):
+        before_first(chunk_at(place))
+    for block in range(4):
+        gather_x(block, 1).wait_recv()
+        if block < 2:
+            gather_relay(block).start()
+        gather_x(block, 0).wait_recv()
+        if block >= 2:
+            gather_relay(block).start()
+    for place in (2, 3):
+        before_first(chunk_at(place))
+    loads[1].wait()
+    for block in range(4):
+        gather_relay(block).wait_recv()
+    loads[3].wait()
+
+    for place in range(SPLIT):
+        c = chunk_at(place)
+        finish_first(c)
+        after(0, c)
+        send(0, c)
+        if place == 0:
+            loads[2].wait()
+        image[pl.ds(layers * c, layers)] = imaged(0, c)
+    before(1, chunk_at(0))
 
     def slot(s, carry):
-        n, c = lax.div(s, SPLIT), lax.rem(s, SPLIT)
-        nxt = 1 - lax.rem(n, 2)
+        n, c = lax.div(s, SPLIT), chunk_of(lax.rem(s, SPLIT))
         after(n, c)
-
-        @pl.when(n < STEPS - 1)
-        def _():
-            each_end(x_ends, lambda side: x_copy(nxt, c, side, None).start())
-            pack_y(nxt, c)
-            each_end(y_ends, lambda side: y_copy(nxt, c, side).start())
-
-        which = slot_ref[STEPS - 1 - n]
+        send(n, c)
         zs = pl.ds(layers * c, layers)
-        image[zs] = image[zs] + saved[which, zs] * (
-            field[nxt, pl.ds(8 + layers * c, layers), pl.ds(8, span_x), :]
-        )
-
-        @pl.when(s + 1 < STEPS * SPLIT)
-        def _():
-            before(lax.div(s + 1, SPLIT), lax.rem(s + 1, SPLIT))
-
+        image[zs] = image[zs] + imaged(n, c)
+        before(lax.div(s + 1, SPLIT), chunk_of(lax.rem(s + 1, SPLIT)))
         return carry
 
-    lax.fori_loop(0, STEPS * SPLIT, slot, 0)
-    end = STEPS % 2
-    result = pltpu.make_async_copy(
-        field.at[end, pl.ds(8, depth), pl.ds(8, span_x), :], out_ref.at[0], load_sem.at[0]
-    )
-    result.start()
+    lax.fori_loop(SPLIT, (STEPS - 1) * SPLIT, slot, 0)
 
     sx = sx_ref[0].astype(F32)
     sy = sy_ref[0].astype(F32)
@@ -399,13 +433,6 @@
     cell_y = (ty * span_y + lax.broadcasted_iota(jnp.int32, (span_x, span_y), 1)).astype(F32) - sy
     flat = cell_x * cell_x + cell_y * cell_y
 
-    def mute(z, carry):
-        gap = z.astype(F32) - src_depth
-        image[z] = image[z] * (1.0 - jnp.exp(-(gap * gap + flat) / (mute_radius * mute_radius)))
-        return carry
-
-    lax.fori_loop(0, depth, mute, 0)
-
     def piece(column_at, q):
         return pl.ds(8 * column_at + 2 * q, 2)
 
@@ -440,14 +467,46 @@
             device_id_type=MESH,
         )
 
-    for q in range(4):
-        sum_far(q).start()
-    for q in range(4):
-        sum_near(q, 0 if q < 2 else 1).start()
-    for q in range(4):
-        sum_far(q).wait_recv()
-        pass_out[q] = pass_in[q] + image[piece(right if q < 2 else left, q)]
-        sum_near(q, 1 if q < 2 else 0).start()
+    results = []
+    for place in range(SPLIT):
+        c = chunk_at(place)
+        after(STEPS - 1, c)
+        zs = pl.ds(layers * c, layers)
+        muted = image[zs] + imaged(STEPS - 1, c)
+        for j in range(layers):
+            gap = (layers * c + j).astype(F32) - src_depth
+            image[layers * c + j] = muted[j] * (
+                1.0 - jnp.exp(-(gap * gap + flat) / (mute_radius * mute_radius))
+            )
+        result = pltpu.make_async_copy(
+            field.at[STEPS % 2, pl.ds(8 + layers * c, layers), pl.ds(8, span_x), :],
+            out_ref.at[0, zs],
+            load_sem.at[place],
+        )
+        result.start()
+        results.append(result)
+        if place == 0:
+            for q in range(4):
+                sum_far(q).start()
+        if place == 1:
+            for q in (2, 3):
+                sum_near(q, 1).start()
+        if place == 2:
+            for q in (0, 1):
+                sum_near(q, 0).start()
+            for q in (0, 1):
+                sum_far(q).wait_recv()
+                pass_out[q] = pass_in[q] + image[piece(right, q)]
+            for q in (0, 1):
+                sum_near(q, 1).start()
+        if place < SPLIT - 1:
+            before(STEPS - 1, chunk_at(place + 1))
+        if place == 2:
+            for q in (2, 3):
+                sum_far(q).wait_recv()
+                pass_out[q] = pass_in[q] + image[piece(left, q)]
+            for q in (2, 3):
+                sum_near(q, 0).start()
     for q in range(4):
         sum_near(q, 0).wait_recv()
         sum_near(q, 1).wait_recv()
@@ -458,9 +517,7 @@
     for distance in (1, 2, 3):
         sum_depth(distance).wait_recv()
         total = total + last_in[distance - 1]
-    gradient = total * F32(1.0 / math.sqrt(lax.axis_size("shot") * STEPS))
-    grad_ref[...] = gradient
-    upd_ref[...] = model_ref[...] - step_size * gradient
+    sum_ref[...] = total
 
     last = (STEPS - 1) % 2
     for c in range(SPLIT):
@@ -475,7 +532,8 @@
         for side in range(2):
             gather_x(q, side).wait_send()
             sum_near(q, side).wait_send()
-    result.wait()
+    for result in results:
+        result.wait()
 
 
 def shards(
@@ -497,15 +555,14 @@
     vmem = pl.BlockSpec(memory_space=pltpu.VMEM)
     smem = pl.BlockSpec(memory_space=pltpu.SMEM)
     dma = pltpu.SemaphoreType.DMA
-    return pl.pallas_call(
+    state, summed = pl.pallas_call(
         kernel,
         out_shape=(
             jax.ShapeDtypeStruct(adjoint_now.shape, F32),
             jax.ShapeDtypeStruct(model.shape, F32),
-            jax.ShapeDtypeStruct(model.shape, F32),
         ),
         in_specs=[anywhere, anywhere, anywhere, vmem, vmem, vmem, smem, smem, smem, vmem],
-        out_specs=(anywhere, vmem, vmem),
+        out_specs=(anywhere, vmem),
         scratch_shapes=[
             pltpu.VMEM((2, depth + 16, span_x + 16, span_y), F32),
             pltpu.VMEM((depth, span_x, span_y), F32),
@@ -541,13 +598,13 @@
             dma((3,)),
         ],
         compiler_params=pltpu.CompilerParams(
-            collective_id=0, has_side_effects=True, vmem_limit_bytes=40 * 1024 * 1024
+            collective_id=0, has_side_effects=True, vmem_limit_bytes=63 * 1024 * 1024
         ),
     )(
         adjoint_prior,
         adjoint_now,
         forward_saved,
-        residuals,
+        jnp.swapaxes(residuals, 0, 1),
         receiver_x,
         receiver_y,
         source_x,
@@ -555,6 +612,8 @@
         saved_slot,
         model,
     )
+    gradient = summed * (1.0 / math.sqrt(lax.axis_size("shot") * STEPS))
+    return state, gradient, model - step_size * gradient
 
 
 def solution(mesh):

time: 111 us -> 105 us (0.946)
  the two profiles are of different devices: /device:TPU:1 before, /device:TPU:17 now
where the time goes in v2:
time: 105 us; the launch traced here: 104 us
  Pallas kernels  99.2 us (94%)
  between operations  1.95 us (2%)
  local copies, waits for them, and re-layouts  1.87 us (2%)
  other arithmetic  1.39 us (1%)
    pallas_call x1, Pallas kernels, shards(): pl.pallas_call(kernel, out_shape=(jax.ShapeDtypeStruct(adjoint_now.shape,...  99.2 us

profile of v2, /device:TPU:17, one launch (start us, length us, event | category | flops | bytes accessed | tf_op | source)
XLA Modules:
  0.0 104.4 jit_solution(16583510661446114601)
XLA Ops:
  1.9 0.0 copy-start
  1.9 99.2 %shard_map.121 = (f32[1,32,32,128]{3,2,1,0:T(8,128)}, f32[2,32,128]{2,1,0:T(8,128)}) custom-call(f32[1,32,32,128]{3,2,1,0:T(8,128)} %prior_ref.1, f32[1,32,32,128]{3,2,1,0:T(8,128)} %now_ref.1, f32[1,2,32,32,128]{4,3,2,1,0:T(8,128)} %fwd_ref.1, f32[10,1,1024]{2,1,0:T(1,128)} %bitcast.1, s32[1,1024]{1,0:T(1,128)} %rx_ref.1, s32[1,1024]{1,0:T(1,128)} %ry_ref.1, ...), custom_call_target="tpu_custom_call" | custom-call | tf_op jit(solution)/shard_map/pallas_call | solution.py:558
  101.1 0.0 copy-done
  101.1 1.4 %multiply_subtract_fusion = (f32[2,32,128]{2,1,0:T(8,128)}, f32[2,32,128]{2,1,0:T(8,128)}) fusion(f32[2,32,128]{2,1,0:T(8,128)S(1)} %copy-done, f32[2,32,128]{2,1,0:T(8,128)} %get-tuple-element.6), kind=kLoop, calls=%fused_computation | loop fusion | flops 24576 | bytes 131072 | tf_op jit(solution)/shard_map/sub | solution.py:616
  102.5 1.9 %copy.16 = f32[1,32,32,128]{3,2,1,0:T(8,128)} copy(f32[1,32,32,128]{3,2,1,0:T(8,128)} %get-tuple-element.12) | data formatting | bytes 1048576
Async XLA Ops:
  1.9 99.2 %copy-start = (f32[2,32,128]{2,1,0:T(8,128)S(1)}, f32[2,32,128]{2,1,0:T(8,128)}, u32[]{:S(2)}) copy-start(f32[2,32,128]{2,1,0:T(8,128)} %model_ref.1) | copy-start | bytes 98308

commit v3 on v2

--- a/solution.py
+++ b/solution.py
@@ -60,6 +60,7 @@
     surface,
     ylap,
     band,
+    comb,
     xin,
     yout,
     yin,
@@ -247,6 +248,15 @@
         band[pl.ds(256 * i + 128, 128), pl.ds(0, 128)] = high
         band[pl.ds(256 * i + 128, 128), pl.ds(128, 128)] = jnp.zeros((128, 128), BF16)
 
+    cells = layers * span_x
+    row = lax.broadcasted_iota(jnp.int32, (cells, cells), 0)
+    column = lax.broadcasted_iota(jnp.int32, (cells, cells), 1)
+    away = jnp.where(lax.div(row, span_x) == lax.div(column, span_x), jnp.abs(row - column), 0)
+    inner = jnp.zeros((cells, cells), F32)
+    for k in range(1, 9):
+        inner = jnp.where(away == k, F32(weights[k - 1]), inner)
+    comb[0], comb[1] = halves(inner)
+
     count = rx_ref.shape[1]
     local_x = rx_ref[...] - tx * span_x
     local_y = ry_ref[...] - ty * span_y
@@ -272,9 +282,6 @@
     def chunk_at(place):
         return lax.rem(col + (2, 1, 3, 0)[place], SPLIT)
 
-    def chunk_of(place):
-        return lax.rem(col + 2 + 3 * place + 3 * lax.div(place * (place - 1), 2), SPLIT)
-
     def stencil(par, c, store):
         base = layers * c
         value = field[par, pl.ds(8 + base, layers), pl.ds(8, span_x), :].reshape(
@@ -293,31 +300,34 @@
             band[...],
             preferred_element_type=F32,
         )
-        ylap[...] = (sides[:, :span_y] + sides[:, span_y:]).reshape(layers, span_x, span_y)
+        across = jnp.dot(
+            comb[0], jnp.concatenate([high, low], axis=1), preferred_element_type=F32
+        )
+        across_low = jnp.dot(comb[1], high, preferred_element_type=F32)
+        both = sides + across
+        ylap[...] = (both[:, :span_y] + both[:, span_y:] + across_low).reshape(
+            layers, span_x, span_y
+        )
         for t in range(tiles):
             rows = pl.ds(8 + 8 * t, 8)
             plane = [field[par, base + i, rows, :] for i in range(layers + 16)]
             made = []
             for j in range(layers):
-                total = ylap[j, pl.ds(8 * t, 8), :]
+                here = plane[8 + j]
+                total = F32(3.0 * centre) * here
                 for k in range(1, 9):
-                    pairs = (plane[8 + j + k] + plane[8 + j - k]) + (
-                        field[par, 8 + base + j, pl.ds(8 + 8 * t + k, 8), :]
-                        + field[par, 8 + base + j, pl.ds(8 + 8 * t - k, 8), :]
-                    )
+                    pairs = plane[8 + j + k] + plane[8 + j - k]
                     total = total + F32(weights[k - 1]) * pairs
-                here = plane[8 + j]
-                made.append((here, total + F32(3.0 * centre) * here))
+                made.append((here, total + ylap[j, pl.ds(8 * t, 8), :]))
             store(t, made)
 
-    def add_receivers(n, c):
+    def add_receivers(n, c, par):
         @pl.when(c == 0)
         def _():
-            at = (1 - lax.rem(n, 2), 8 + rec_depth, pl.ds(8, span_x))
+            at = (1 - par, 8 + rec_depth, pl.ds(8, span_x))
             field[at] = field[at] + surface[STEPS - 1 - n]
 
-    def before(n, c):
-        par = lax.rem(n, 2)
+    def before(n, c, par):
         each_end(x_ends, lambda side: x_copy(1 - par, c, side, None).wait_send())
         each_end(y_ends, lambda side: y_copy(1 - par, c, side).wait_send())
         each_end(y_ends, lambda side: y_copy(par, c, 1 - side).wait_recv())
@@ -335,7 +345,7 @@
                 field[1 - par, 8 + base + j, rows, :] = new[j]
 
         stencil(par, c, store)
-        add_receivers(n, c)
+        add_receivers(n, c, par)
 
     def before_first(c):
         each_end(y_ends, lambda side: y_copy(0, c, 1 - side).wait_recv())
@@ -353,10 +363,9 @@
         field[(1,) + inside] = (
             2.0 * field[(0,) + inside] - field[(1,) + inside] + speed[zs] * image[zs]
         )
-        add_receivers(0, c)
-
-    def after(n, c):
-        par = lax.rem(n, 2)
+        add_receivers(0, c, 0)
+
+    def after(c, par):
         base = layers * c
         each_end(x_ends, lambda side: x_copy(par, c, 1 - side, None).wait_recv())
         for side in range(2):
@@ -375,15 +384,14 @@
             for j in range(layers):
                 field[1 - par, 8 + base + j, rows, :] = new[j]
 
-    def send(n, c):
-        nxt = 1 - lax.rem(n, 2)
+    def send(c, nxt):
         each_end(x_ends, lambda side: x_copy(nxt, c, side, None).start())
         pack_y(nxt, c)
         each_end(y_ends, lambda side: y_copy(nxt, c, side).start())
 
-    def imaged(n, c):
+    def imaged(n, c, nxt):
         zs = pl.ds(layers * c, layers)
-        inside = (1 - lax.rem(n, 2), pl.ds(8 + layers * c, layers), pl.ds(8, span_x))
+        inside = (nxt, pl.ds(8 + layers * c, layers), pl.ds(8, span_x))
         return saved[slot_ref[STEPS - 1 - n], zs] * field[inside]
 
     for block in (1, 2, 3):
@@ -409,23 +417,30 @@
     for place in range(SPLIT):
         c = chunk_at(place)
         finish_first(c)
-        after(0, c)
-        send(0, c)
+        after(c, 0)
+        send(c, 1)
         if place == 0:
             loads[2].wait()
-        image[pl.ds(layers * c, layers)] = imaged(0, c)
-    before(1, chunk_at(0))
-
-    def slot(s, carry):
-        n, c = lax.div(s, SPLIT), chunk_of(lax.rem(s, SPLIT))
-        after(n, c)
-        send(n, c)
-        zs = pl.ds(layers * c, layers)
-        image[zs] = image[zs] + imaged(n, c)
-        before(lax.div(s + 1, SPLIT), chunk_of(lax.rem(s + 1, SPLIT)))
+        image[pl.ds(layers * c, layers)] = imaged(0, c, 1)
+    before(1, chunk_at(0), 1)
+
+    def two_steps(pair, carry):
+        for half in range(2):
+            n = 1 + 2 * pair + half
+            par = 1 - half
+            for place in range(SPLIT):
+                c = chunk_at(place)
+                after(c, par)
+                send(c, 1 - par)
+                zs = pl.ds(layers * c, layers)
+                image[zs] = image[zs] + imaged(n, c, 1 - par)
+                if place < SPLIT - 1:
+                    before(n, chunk_at(place + 1), par)
+                else:
+                    before(n + 1, chunk_at(0), 1 - par)
         return carry
 
-    lax.fori_loop(SPLIT, (STEPS - 1) * SPLIT, slot, 0)
+    lax.fori_loop(0, (STEPS - 2) // 2, two_steps, 0)
 
     sx = sx_ref[0].astype(F32)
     sy = sy_ref[0].astype(F32)
@@ -470,9 +485,9 @@
     results = []
     for place in range(SPLIT):
         c = chunk_at(place)
-        after(STEPS - 1, c)
+        after(c, (STEPS - 1) % 2)
         zs = pl.ds(layers * c, layers)
-        muted = image[zs] + imaged(STEPS - 1, c)
+        muted = image[zs] + imaged(STEPS - 1, c, STEPS % 2)
         for j in range(layers):
             gap = (layers * c + j).astype(F32) - src_depth
             image[layers * c + j] = muted[j] * (
@@ -500,7 +515,7 @@
             for q in (0, 1):
                 sum_near(q, 1).start()
         if place < SPLIT - 1:
-            before(STEPS - 1, chunk_at(place + 1))
+            before(STEPS - 1, chunk_at(place + 1), (STEPS - 1) % 2)
         if place == 2:
             for q in (2, 3):
                 sum_far(q).wait_recv()
@@ -571,6 +586,7 @@
             pltpu.VMEM((STEPS, span_x, span_y), F32),
             pltpu.VMEM((layers, span_x, span_y), F32),
             pltpu.VMEM((512, 256), BF16),
+            pltpu.VMEM((2, layers * span_x, layers * span_x), BF16),
             pltpu.VMEM((2, SPLIT, 2, layers, 16, span_y), F32),
             pltpu.VMEM((2, SPLIT, tiles, 8, span_y), F32),
             pltpu.VMEM((2, SPLIT, 2, tiles, 8, span_y), F32),

time: 105 us -> 104 us (level)
  the two profiles are of different devices: /device:TPU:17 before, /device:TPU:9 now
where the time goes in v3:
time: 104 us
  Pallas kernels  98.8 us (95%)
  between operations  1.95 us (2%)
  local copies, waits for them, and re-layouts  1.87 us (2%)
  other arithmetic  1.39 us (1%)
    pallas_call x1, Pallas kernels, shards(): pl.pallas_call(kernel, out_shape=(jax.ShapeDtypeStruct(adjoint_now.shape,...  98.8 us

profile of v3, /device:TPU:9, one launch (start us, length us, event | category | flops | bytes accessed | tf_op | source)
XLA Modules:
  0.0 104.0 jit_solution(15769018750467269376)
XLA Ops:
  1.9 0.0 copy-start
  1.9 98.8 %shard_map.121 = (f32[1,32,32,128]{3,2,1,0:T(8,128)}, f32[2,32,128]{2,1,0:T(8,128)}) custom-call(f32[1,32,32,128]{3,2,1,0:T(8,128)} %prior_ref.1, f32[1,32,32,128]{3,2,1,0:T(8,128)} %now_ref.1, f32[1,2,32,32,128]{4,3,2,1,0:T(8,128)} %fwd_ref.1, f32[10,1,1024]{2,1,0:T(1,128)} %bitcast.1, s32[1,1024]{1,0:T(1,128)} %rx_ref.1, s32[1,1024]{1,0:T(1,128)} %ry_ref.1, ...), custom_call_target="tpu_custom_call" | custom-call | tf_op jit(solution)/shard_map/pallas_call | solution.py:573
  100.8 0.0 copy-done
  100.8 1.4 %multiply_subtract_fusion = (f32[2,32,128]{2,1,0:T(8,128)}, f32[2,32,128]{2,1,0:T(8,128)}) fusion(f32[2,32,128]{2,1,0:T(8,128)S(1)} %copy-done, f32[2,32,128]{2,1,0:T(8,128)} %get-tuple-element.6), kind=kLoop, calls=%fused_computation | loop fusion | flops 24576 | bytes 131072 | tf_op jit(solution)/shard_map/sub | solution.py:632
  102.2 1.9 %copy.16 = f32[1,32,32,128]{3,2,1,0:T(8,128)} copy(f32[1,32,32,128]{3,2,1,0:T(8,128)} %get-tuple-element.12) | data formatting | bytes 1048576
Async XLA Ops:
  1.9 98.9 %copy-start = (f32[2,32,128]{2,1,0:T(8,128)S(1)}, f32[2,32,128]{2,1,0:T(8,128)}, u32[]{:S(2)}) copy-start(f32[2,32,128]{2,1,0:T(8,128)} %model_ref.1) | copy-start | bytes 98308

commit v4 on v3

--- a/solution.py
+++ b/solution.py
@@ -365,12 +365,11 @@
         )
         add_receivers(0, c, 0)
 
-    def after(c, par):
+    def after(c, par, onward=True):
         base = layers * c
-        each_end(x_ends, lambda side: x_copy(par, c, 1 - side, None).wait_recv())
-        for side in range(2):
-            t = (tiles - 1) * side
-            rows = pl.ds(8 + 8 * t, 8)
+
+        def outer_tile(side):
+            rows = pl.ds(8 + (span_x - 8) * side, 8)
             new = []
             for j in range(layers):
                 total = jnp.zeros((8, span_y), F32)
@@ -379,13 +378,25 @@
                     total = total + F32(weights[k - 1]) * xin[par, c, side, j, pl.ds(start, 8), :]
                 new.append(
                     field[1 - par, 8 + base + j, rows, :]
-                    + speed[base + j, pl.ds(8 * t, 8), :] * total
+                    + speed[base + j, pl.ds((span_x - 8) * side, 8), :] * total
                 )
             for j in range(layers):
                 field[1 - par, 8 + base + j, rows, :] = new[j]
 
+        for parity in range(2):
+
+            @pl.when(lax.rem(tx, 2) == parity)
+            def _(parity=parity):
+                for side in (parity, 1 - parity):
+
+                    @pl.when(x_ends[side][0])
+                    def _(side=side):
+                        x_copy(par, c, 1 - side, None).wait_recv()
+                        outer_tile(side)
+                        if onward:
+                            x_copy(1 - par, c, side, None).start()
+
     def send(c, nxt):
-        each_end(x_ends, lambda side: x_copy(nxt, c, side, None).start())
         pack_y(nxt, c)
         each_end(y_ends, lambda side: y_copy(nxt, c, side).start())
 
@@ -485,7 +496,7 @@
     results = []
     for place in range(SPLIT):
         c = chunk_at(place)
-        after(c, (STEPS - 1) % 2)
+        after(c, (STEPS - 1) % 2, onward=False)
         zs = pl.ds(layers * c, layers)
         muted = image[zs] + imaged(STEPS - 1, c, STEPS % 2)
         for j in range(layers):

time: 104 us -> 104 us (level)
  no operation moved by 1% of the time
where the time goes in v4:
time: 104 us
  Pallas kernels  98.5 us (95%)
  between operations  1.95 us (2%)
  local copies, waits for them, and re-layouts  1.87 us (2%)
  other arithmetic  1.39 us (1%)
    pallas_call x1, Pallas kernels, shards(): pl.pallas_call(kernel, out_shape=(jax.ShapeDtypeStruct(adjoint_now.shape,...  98.5 us

profile of v4, /device:TPU:9, one launch (start us, length us, event | category | flops | bytes accessed | tf_op | source)
XLA Modules:
  0.0 103.7 jit_solution(13097566757941276654)
XLA Ops:
  1.9 0.0 copy-start
  1.9 98.5 %shard_map.121 = (f32[1,32,32,128]{3,2,1,0:T(8,128)}, f32[2,32,128]{2,1,0:T(8,128)}) custom-call(f32[1,32,32,128]{3,2,1,0:T(8,128)} %prior_ref.1, f32[1,32,32,128]{3,2,1,0:T(8,128)} %now_ref.1, f32[1,2,32,32,128]{4,3,2,1,0:T(8,128)} %fwd_ref.1, f32[10,1,1024]{2,1,0:T(1,128)} %bitcast.1, s32[1,1024]{1,0:T(1,128)} %rx_ref.1, s32[1,1024]{1,0:T(1,128)} %ry_ref.1, ...), custom_call_target="tpu_custom_call" | custom-call | tf_op jit(solution)/shard_map/pallas_call | solution.py:584
  100.4 0.0 copy-done
  100.4 1.4 %multiply_subtract_fusion = (f32[2,32,128]{2,1,0:T(8,128)}, f32[2,32,128]{2,1,0:T(8,128)}) fusion(f32[2,32,128]{2,1,0:T(8,128)S(1)} %copy-done, f32[2,32,128]{2,1,0:T(8,128)} %get-tuple-element.6), kind=kLoop, calls=%fused_computation | loop fusion | flops 24576 | bytes 131072 | tf_op jit(solution)/shard_map/sub | solution.py:643
  101.8 1.9 %copy.16 = f32[1,32,32,128]{3,2,1,0:T(8,128)} copy(f32[1,32,32,128]{3,2,1,0:T(8,128)} %get-tuple-element.12) | data formatting | bytes 1048576
Async XLA Ops:
  1.9 98.5 %copy-start = (f32[2,32,128]{2,1,0:T(8,128)S(1)}, f32[2,32,128]{2,1,0:T(8,128)}, u32[]{:S(2)}) copy-start(f32[2,32,128]{2,1,0:T(8,128)} %model_ref.1) | copy-start | bytes 98308
